TPU v7x, 32 devices: a whole 2x2x4 slice. The times are simulated.
32 devices in a mesh: sec: 2 (over core), gx: 4 (over z), gy: 4 (over y, x).
Axes of the slice: x: 2, y: 2, z: 4, core: 2. Of those that a mesh axis runs over, the one named last changes fastest.
Arguments:
- slide_thickness: float32 [8, 4, 128, 512], P(('sec', 'gy'), 'gx'), may hold values from 0.2 to 2
- footprint: int32 [8, 4, 128, 512], P(('sec', 'gy'), 'gx'), may hold values 0 or 1
- slide_momentum: float32 [8, 4, 128, 512], P(('sec', 'gy'), 'gx'), may hold values from -1.5 to 1.5
- bed_friction: float32 [8, 4, 128, 512], P(('sec', 'gy'), 'gx'), may hold values from 0.1 to 1
- surface: float32 [4096, 512], P(('sec', 'gy'), 'gx'), may hold values from -2 to 2
- flux_x: float32 [3, 4096, 512], P(None, ('sec', 'gy'), 'gx'), may hold values from -2 to 2
- flux_y: float32 [3, 4096, 512], P(None, ('sec', 'gy'), 'gx'), may hold values from -2 to 2
- bathy_class: int32 [4096, 512], P(('sec', 'gy'), 'gx'), may hold values from 0 to 7
- depth_table: float32 [8], replicated, may hold values from 2 to 8
Outputs:
- surface_out: float32 [4096, 512], P(('sec', 'gy'), 'gx')
- pressure_out: float32 [3, 4096, 512], P(None, ('sec', 'gy'), 'gx')
- bottom_load: float32 [8, 4, 128, 512], P(('sec', 'gy'), 'gx')
- thickness_out: float32 [512, 4096], P(('sec', 'gx', 'gy'))
- momentum_out: float32 [512, 4096], P(('sec', 'gx', 'gy'))
All inputs are finite; a program needn't handle non-finite values. No bound on the sum of `footprint` on one device may be relied on, other than what follows from the above.
Results may differ from a plain program's by a relative error of at most 0.0001.
Values sent between devices are 32-bit elements; how exact they have to be, the bound alone decides.
No kernel may reach another device: no remote copies, remote signals or barrier semaphores. Data moves between devices by JAX's collectives and lax.ppermute only.
A program may use at most 128 MiB of HBM per device.

v0:
```python
import functools

import jax
import jax.numpy as jnp
from jax import lax
from jax.experimental import pallas as pl
from jax.experimental.pallas import tpu as pltpu
from jax.sharding import PartitionSpec as P

LEVELS = 4
SWEEPS = 4
LAYERS = 3

GRAVITY_PUSH = 0.4
SPREAD = 0.25
SOURCE = 2.0
SURFACE_STEP = 0.2
COURANT = 0.25
SLOPE_PULL = 0.5
LAYER_SHARE = (0.2, 0.3, 0.5)

STEP = SWEEPS + 3
RIM = LEVELS * STEP
EDGE = 32
LANES = 128
TOP = 8
F32 = jnp.float32


def smem():
    return pl.BlockSpec(memory_space=pltpu.SMEM)


def vmem():
    return pl.BlockSpec(memory_space=pltpu.VMEM)


def call(kernel, scalars, inputs, outs, scratch=(), flops=10**6, moved=10**6, name=None):
    return pl.pallas_call(
        kernel,
        out_shape=[jax.ShapeDtypeStruct(s, F32) for s in outs],
        in_specs=[smem()] * len(scalars) + [vmem()] * len(inputs),
        out_specs=[vmem() for _ in outs],
        scratch_shapes=list(scratch),
        cost_estimate=pl.CostEstimate(flops=flops, bytes_accessed=moved, transcendentals=0),
        name=name,
    )(*scalars, *inputs)


def lane_of(shape):
    return lax.broadcasted_iota(jnp.int32, shape, len(shape) - 1)


def row_of(shape):
    return lax.broadcasted_iota(jnp.int32, shape, len(shape) - 2)


def pack_slide_kernel(n, tile_x, where_ref, th, fp, mo, fr, *rest):
    blocks, turned = rest[:n], rest[n]
    cells_x = th.shape[1]
    deep = tile_x + 2 * RIM
    g = where_ref[0]
    fields = (
        lambda cols: th[:, cols] * fp[:, cols].astype(F32),
        lambda cols: mo[:, cols],
        lambda cols: fr[:, cols],
    )
    for a, field in enumerate(fields):
        turned[a, :RIM, :] = jnp.zeros((RIM, LANES), F32)
        turned[a, RIM + cells_x :, :] = jnp.zeros((RIM, LANES), F32)
        for i in range(cells_x // LANES):
            turned[a, RIM + i * LANES : RIM + (i + 1) * LANES, :] = field(
                slice(i * LANES, (i + 1) * LANES)
            ).T
    for shift in range(n):
        start = pl.multiple_of(lax.rem(g + shift, n) * tile_x, 8)
        for a in range(3):
            blocks[shift][a * deep : (a + 1) * deep, :] = turned[a, pl.ds(start, deep), :]


def slide_kernel(th, fp, mo, fr, out_h, out_m, hs, ms):
    w, cells = th.shape
    lane = lane_of((8, cells))

    def body(c, carry):
        rows = pl.ds(pl.multiple_of(c * 8, 8), 8)
        h = th[rows, :] * fp[rows, :].astype(F32)
        m = mo[rows, :]
        f = fr[rows, :]

        def lo(v):
            return jnp.where(lane == 0, 0.0, pltpu.roll(v, 1, 1))

        def hi(v):
            return jnp.where(lane == cells - 1, 0.0, pltpu.roll(v, cells - 1, 1))

        for _ in range(LEVELS):
            u = m / (1.0 + jnp.abs(h))
            carry_m = m * u + 0.5 * h * h
            drag = f * h * u / jnp.sqrt(u * u + 1.0)
            m_lo, m_hi = lo(m), hi(m)
            new_h = 0.5 * (lo(h) + hi(h)) - 0.5 * COURANT * (m_hi - m_lo)
            m = (
                0.5 * (m_lo + m_hi)
                - 0.5 * COURANT * (hi(carry_m) - lo(carry_m))
                + COURANT * (SLOPE_PULL * h - drag)
            )
            h = new_h
        hs[rows, :] = h
        ms[rows, :] = m
        return carry

    lax.fori_loop(0, w // 8, body, 0)
    for i in range(cells // LANES):
        cols = slice(i * LANES, (i + 1) * LANES)
        out_h[cols, :] = hs[:, cols].T
        out_m[cols, :] = ms[:, cols].T


def pack_wave_kernel(table, eta, fx, fy, cls, low, high, wide, edge_u, v_pad):
    tile_y, tile_x = eta.shape
    count = table.shape[0]
    lane = lane_of((LANES, tile_x))
    v_pad[:, :8, :] = jnp.zeros((LAYERS, 8, tile_x), F32)
    v_pad[:, 8 + tile_y :, :] = jnp.zeros((LAYERS, 8, tile_x), F32)
    for k in range(LAYERS):
        v_pad[k, 8 : 8 + tile_y, :] = fy[k]
    last = tile_y // LANES - 1
    for i in range(tile_y // LANES):
        rows = slice(i * LANES, (i + 1) * LANES)

        def keep(a, value, turned=True):
            if i == 0:
                low[a * EDGE : (a + 1) * EDGE, :] = value[:EDGE]
            if i == last:
                high[a * EDGE : (a + 1) * EDGE, :] = value[LANES - EDGE :]
            if a < 5:
                wide[a, :, rows] = value.T
            else:
                edge_u[:, rows] = value.T[:8]

        keep(0, eta[rows, :])
        ends = jnp.zeros((LANES, tile_x), F32)
        for k in range(LAYERS):
            u = fx[k, rows, :]
            right = jnp.where(lane == tile_x - 1, 0.0, pltpu.roll(u, tile_x - 1, 1))
            left = jnp.where(lane == 0, 0.0, pltpu.roll(u, 1, 1))
            up = v_pad[k, 9 + i * LANES : 9 + (i + 1) * LANES, :]
            down = v_pad[k, 7 + i * LANES : 7 + (i + 1) * LANES, :]
            keep(1 + k, 2.0 * ((right - left) + (up - down)))
            head = u if k == 0 else pltpu.roll(u, k, 1)
            ends = jnp.where(lane == k, head, ends)
            ends = jnp.where(lane == LAYERS + k, pltpu.roll(u, LAYERS + k + 1, 1), ends)
        found = cls[rows, :]
        depth = jnp.zeros((LANES, tile_x), F32)
        for j in range(count):
            depth = jnp.where(found == j, table[j], depth)
        keep(4, depth)
        keep(5, ends)
    base = 6 * EDGE
    low[base:, :] = jnp.zeros((8, tile_x), F32)
    high[base:, :] = jnp.zeros((8, tile_x), F32)
    for k in range(LAYERS):
        low[base + k : base + k + 1, :] = fy[k, 0:1, :]
        high[base + k : base + k + 1, :] = fy[k, tile_y - 1 : tile_y, :]


def widen_wave_kernel(where_ref, wide, edge_u, low, high, from_low, from_high, out, out_u, send_a, send_b):
    g, b, nb = where_ref[0], where_ref[1], where_ref[3]
    tile_x, tile_y = wide.shape[1:]
    tiles = tile_y // LANES
    has_low = (b > 0).astype(F32)
    has_high = (b < nb - 1).astype(F32)
    row = row_of((EDGE, tile_x))
    lane = lane_of((tile_x, LANES))
    row_full = row_of((LANES, tile_x))
    base = 6 * EDGE
    gap = jnp.zeros((LANES - 2 * EDGE, tile_x), F32)
    for a in range(6):
        up = from_high[a * EDGE : (a + 1) * EDGE, :]
        down = from_low[a * EDGE : (a + 1) * EDGE, :]
        if a == 0:
            up = up * has_high
            down = down * has_low
        if 1 <= a <= LAYERS:
            v_top = high[base + a - 1 : base + a, :]
            v_bottom = low[base + a - 1 : base + a, :]
            up = up - jnp.where(row == 0, 2.0 * v_top, 0.0)
            down = down + jnp.where(row == EDGE - 1, 2.0 * v_bottom, 0.0)
        extra = jnp.concatenate([up, gap, down], axis=0).T
        if a == 5:
            for t in range(tiles):
                out_u[t] = edge_u[:, t * LANES : (t + 1) * LANES]
            out_u[tiles] = extra[:8]
            continue
        out[a, tiles] = extra
        for t in range(tiles):
            out[a, t] = wide[a, :, t * LANES : (t + 1) * LANES]
        if 1 <= a <= LAYERS:
            v_above = from_high[base + a - 1 : base + a, :] * (2.0 * has_high)
            v_below = from_low[base + a - 1 : base + a, :] * (2.0 * has_low)
            fix = jnp.where(row_full == LANES - 1, v_above, jnp.where(row_full == 0, -v_below, 0.0)).T
            out[a, tiles - 1] = out[a, tiles - 1] + jnp.where(lane == LANES - 1, fix, 0.0)
            out[a, 0] = out[a, 0] + jnp.where(lane == 0, fix, 0.0)

    def fill(send, right):
        for t in range(tiles + 1):
            for a in range(5):
                at = (t * 5 + a) * RIM
                rows = slice(tile_x - RIM, tile_x) if right else slice(0, RIM)
                send[at : at + RIM, :] = out[a, t, rows, :]
            at = (tiles + 1) * 5 * RIM + t * 4
            rows = slice(LAYERS, LAYERS + 4) if right else slice(0, 4)
            send[at : at + 4, :] = out_u[t, rows, :]

    even = lax.rem(g, 2) == 0

    @pl.when(even)
    def _():
        fill(send_a, True)
        fill(send_b, False)

    @pl.when(jnp.logical_not(even))
    def _():
        fill(send_a, False)
        fill(send_b, True)


def slide_edge_kernel(n, w, where_ref, *refs):
    blocks = refs[:n]
    low, high, head, tail = refs[n:]
    g = where_ref[0]
    rows = blocks[0].shape[0]
    part = low.shape[0]
    head[rows:, :] = jnp.zeros((head.shape[0] - rows, LANES), F32)
    tail[rows:, :] = jnp.zeros((tail.shape[0] - rows, LANES), F32)
    for shift in range(n):

        @pl.when(g == shift)
        def _():
            head[:rows, :] = blocks[shift][...]

        @pl.when(lax.rem(g + 1, n) == shift)
        def _():
            tail[:rows, :] = blocks[shift][...]

    lane = lane_of((part, LANES))
    packed_low = jnp.zeros((part, LANES), F32)
    packed_high = jnp.zeros((part, LANES), F32)
    for p in range(LANES // EDGE):
        here = (lane >= p * EDGE) & (lane < (p + 1) * EDGE)
        v = head[p * part : (p + 1) * part, :]
        turn = (p * EDGE) % LANES
        packed_low = jnp.where(here, pltpu.roll(v, turn, 1) if turn else v, packed_low)
        v = tail[p * part : (p + 1) * part, :]
        turn = (p * EDGE - (w - EDGE)) % LANES
        packed_high = jnp.where(here, pltpu.roll(v, turn, 1) if turn else v, packed_high)
    low[...] = packed_low
    high[...] = packed_high


def wave_kernel(n, w, cells_x, cells_y, where_ref, *refs):
    (wide, edge_u, got_a, got_b, slide_low, slide_high) = refs[:6]
    blocks = refs[6 : 6 + n]
    loads = refs[6 + n : 6 + 2 * n]
    fields_out = refs[6 + 2 * n]
    (eta, div, src, pa, pb, coef, corner, hs, ms, fs, qs, rise, load, stage, left, right) = refs[
        7 + 2 * n :
    ]
    g, b = where_ref[0], where_ref[1]
    tiles, tile_x = wide.shape[1] - 1, wide.shape[2]
    every = range(tiles + 1)
    tile_y = tiles * LANES
    deep = tile_x + 2 * RIM
    total = TOP + deep + TOP
    own = TOP + RIM

    even = lax.rem(g, 2) == 0

    @pl.when(even)
    def _():
        right[...] = got_a[...]
        left[...] = got_b[...]

    @pl.when(jnp.logical_not(even))
    def _():
        left[...] = got_a[...]
        right[...] = got_b[...]

    blank = jnp.zeros((TOP, LANES), F32)
    for t in every:
        for ref in (eta, hs.at[0], hs.at[1], ms.at[0], ms.at[1], qs):
            ref[t, :TOP, :] = blank
            ref[t, total - TOP :, :] = blank
        for k in range(LAYERS):
            for ref in (pa.at[k], pb.at[k]):
                ref[t, :TOP, :] = blank
                ref[t, total - TOP :, :] = blank
        for a, ref in enumerate((eta, div.at[0], div.at[1], div.at[2], corner)):
            at = (t * 5 + a) * RIM
            ref[t, own - RIM : own, :] = left[at : at + RIM, :]
            ref[t, own : own + tile_x, :] = wide[a, t]
            ref[t, own + tile_x : own + tile_x + RIM, :] = right[at : at + RIM, :]
        base = (tiles + 1) * 5 * RIM + t * 4
        end = own + tile_x
        for k in range(LAYERS):
            d = div.at[k]

            def bump(at, value):
                d[t, at : at + 1, :] = d[t, at : at + 1, :] + 2.0 * value

            bump(end - 1, right[base + k : base + k + 1, :])
            bump(end, -edge_u[t, LAYERS + k : LAYERS + k + 1, :])
            bump(own, -left[base + k : base + k + 1, :])
            bump(own - 1, edge_u[t, k : k + 1, :])

    slides = (hs.at[0], ms.at[0], fs)
    if w == LANES:
        for shift in range(n):
            q = lax.rem(g - shift + n, n)
            for a, ref in enumerate(slides):
                ref[q, TOP : TOP + deep, :] = blocks[shift][a * deep : (a + 1) * deep, :]
    else:
        per = LANES // w
        lane_d = lane_of((deep, LANES))
        for a, ref in enumerate(slides):
            for shift in range(n):
                stage[lax.rem(g - shift + n, n), :deep, :] = blocks[shift][a * deep : (a + 1) * deep, :]
            for t in range(tiles):
                v = stage[t * per, :deep, :]
                for j in range(1, per):
                    v = jnp.where(
                        lane_d < j * w, v, pltpu.roll(stage[t * per + j, :deep, :], j * w, 1)
                    )
                ref[t, TOP : TOP + deep, :] = v
    part = slide_low.shape[0]
    lane_p = lane_of((part, LANES))
    for p in range(LANES // EDGE):
        turn = (-p * EDGE) % LANES
        up = slide_high[...]
        up = pltpu.roll(up, turn, 1) if turn else up
        turn = (LANES - EDGE - p * EDGE) % LANES
        down = slide_low[...]
        down = pltpu.roll(down, turn, 1) if turn else down
        stage[0, p * part : (p + 1) * part, :] = jnp.where(
            lane_p < EDGE, up, jnp.where(lane_p >= LANES - EDGE, down, 0.0)
        )
    for a, ref in enumerate(slides):
        ref[tiles, TOP : TOP + deep, :] = stage[0, a * deep : (a + 1) * deep, :]

    lane = lane_of((8, LANES))
    row = row_of((8, LANES))

    def y_of(t):
        local = lane + t * LANES
        if t == tiles:
            local = jnp.where(lane < EDGE, local, lane - LANES)
        return local + b * tile_y

    def y_in(t):
        y = y_of(t)
        return (y >= 0) & (y < cells_y) & ((lane < EDGE) | (lane >= LANES - EDGE))

    def x_in(c):
        x = row + (c * 8 - RIM) + g * tile_x
        return (x >= 0) & (x < cells_x)

    def masked(c, t, value):
        mine = c * 8 >= RIM and c * 8 + 8 <= RIM + tile_x
        if not mine:
            value = jnp.where(x_in(c), value, 0.0)
        if t == tiles:
            value = jnp.where(y_in(t), value, 0.0)
        return value

    def coefficients(c, carry):
        at = pl.ds(pl.multiple_of(TOP + c * 8, 8), 8)
        x = row + (c * 8 - RIM) + g * tile_x
        x_ok = (x >= 0) & (x < cells_x)
        x_ends = 4.0 - (x == 0).astype(F32) - (x == cells_x - 1).astype(F32)
        for t in every:
            y = y_of(t)
            inside = x_ok & y_in(t) if t == tiles else x_ok
            depth = jnp.where(inside, corner[t, at, :], 1.0)
            k = 9.0 / (depth * depth)
            p1 = 1.0 / (1.0 + 3.0 * k)
            l1 = k * p1
            p2 = 1.0 / ((1.0 + 2.0 * k) - k * l1)
            l2 = k * p2
            p3 = 1.0 / ((1.0 + k) - k * l2)
            coef[0, t, at, :] = l1
            coef[1, t, at, :] = l2
            coef[2, t, at, :] = jnp.where(inside, SPREAD * p1, 0.0)
            coef[3, t, at, :] = jnp.where(inside, SPREAD * p2, 0.0)
            coef[4, t, at, :] = jnp.where(inside, SPREAD * p3, 0.0)
            corner[t, at, :] = x_ends - (y == 0).astype(F32) - (y == cells_y - 1).astype(F32)
        return carry

    lax.fori_loop(0, deep // 8, coefficients, 0)

    def chunks(width):
        width = min(width, RIM)
        return range((RIM - width) // 8, -(-(RIM + tile_x + width) // 8))

    def rows(ref, t, c, by=0):
        return ref[t, TOP + c * 8 + by : TOP + c * 8 + by + 8, :]

    def put(ref, t, c, value):
        ref[t, TOP + c * 8 : TOP + c * 8 + 8, :] = value

    def around(ref, c, reach):
        mid = [rows(ref, t, c) for t in every]
        fore = [pltpu.roll(v, reach, 1) for v in mid]
        back = [pltpu.roll(v, LANES - reach, 1) for v in mid]
        ring = []
        for t in every:
            west = jnp.where(lane < reach, fore[t - 1], fore[t])
            east = jnp.where(lane >= LANES - reach, back[(t + 1) % (tiles + 1)], back[t])
            ring.append((west + east) + (rows(ref, t, c, -reach) + rows(ref, t, c, reach)))
        return mid, ring

    def solve(t, c, g1, g2, g3, out):
        l1, l2 = rows(coef.at[0], t, c), rows(coef.at[1], t, c)
        g2 = g2 + l1 * g1
        g3 = g3 + l2 * g2
        x3 = rows(coef.at[4], t, c) * g3
        x2 = rows(coef.at[3], t, c) * g2 + l2 * x3
        x1 = rows(coef.at[2], t, c) * g1 + l1 * x2
        put(out.at[0], t, c, x1)
        put(out.at[1], t, c, x2)
        put(out.at[2], t, c, x3)

    for level in range(LEVELS):
        reach = (LEVELS - level) * STEP
        h_now, h_new = hs.at[level % 2], hs.at[(level + 1) % 2]
        m_now, m_new = ms.at[level % 2], ms.at[(level + 1) % 2]
        moving = level < LEVELS - 1
        if moving:
            for c in chunks(reach):
                for t in every:
                    h, m = rows(h_now, t, c), rows(m_now, t, c)
                    u = m / (1.0 + jnp.abs(h))
                    put(qs, t, c, m * u + 0.5 * h * h)
                    drag = rows(fs, t, c) * h * u * lax.rsqrt(u * u + 1.0)
                    put(m_new, t, c, COURANT * (SLOPE_PULL * h - drag))
        for c in chunks(reach - 1):
            for t in every:
                h = rows(h_now, t, c)
                m_lo, m_hi = rows(m_now, t, c, -1), rows(m_now, t, c, 1)
                h_lo, h_hi = rows(h_now, t, c, -1), rows(h_now, t, c, 1)
                fresh = 0.5 * (h_lo + h_hi) - 0.5 * COURANT * (m_hi - m_lo)
                mine = c * 8 >= RIM and c * 8 + 8 <= RIM + tile_x
                if not mine:
                    fresh = jnp.where(x_in(c), fresh, 0.0)
                put(rise, t, c, fresh - h)
                if moving:
                    q_lo, q_hi = rows(qs, t, c, -1), rows(qs, t, c, 1)
                    moved = (0.5 * (m_lo + m_hi) - 0.5 * COURANT * (q_hi - q_lo)) + rows(m_new, t, c)
                    if not mine:
                        moved = jnp.where(x_in(c), moved, 0.0)
                    put(h_new, t, c, fresh)
                    put(m_new, t, c, moved)
        for c in chunks(reach - 2):
            mid, ring = around(eta, c, 2)
            for t in every:
                push = GRAVITY_PUSH * (ring[t] - rows(corner, t, c) * mid[t])
                up = rows(rise, t, c)
                vector = []
                for k in range(LAYERS):
                    d = rows(div.at[k], t, c) - push
                    put(div.at[k], t, c, d)
                    s = (4.0 * SOURCE * LAYER_SHARE[k]) * up - d
                    put(src.at[k], t, c, s)
                    vector.append(s)
                if level == 0:
                    solve(t, c, *vector, pb)
        done = 1 if level == 0 else 0
        for sweep in range(done, SWEEPS):
            old, new = (pa, pb) if sweep % 2 == 0 else (pb, pa)
            for c in chunks(reach - 2 - sweep):
                rings = [around(old.at[k], c, 1)[1] for k in range(LAYERS)]
                for t in every:
                    solve(t, c, *(rings[k][t] + rows(src.at[k], t, c) for k in range(LAYERS)), new)
        press = pa if SWEEPS % 2 == 0 else pb
        for c in chunks(reach - STEP):
            flow = None
            for k in range(LAYERS):
                mid, ring = around(press.at[k], c, 2)
                ds = [
                    rows(div.at[k], t, c) - SPREAD * (ring[t] - rows(corner, t, c) * mid[t])
                    for t in every
                ]
                if moving:
                    for t in every:
                        put(div.at[k], t, c, ds[t])
                flow = ds if flow is None else [f + d for f, d in zip(flow, ds)]
            for t in every:
                change = rows(rise, t, c) - (0.25 * SURFACE_STEP) * flow[t]
                put(eta, t, c, rows(eta, t, c) + masked(c, t, change))
        for c in chunks(0):
            for t in range(tiles):
                bottom = rows(press.at[LAYERS - 1], t, c)
                if level > 0:
                    bottom = rows(load, t, c) + bottom
                put(load, t, c, bottom * (1.0 / LEVELS) if level == LEVELS - 1 else bottom)
    for q in range(n):
        for shift in range(n):

            @pl.when(lax.rem(g + shift, n) == q)
            def _():
                turned = load[q * w // LANES, own : own + tile_x, :].T
                loads[shift][...] = turned[q * w % LANES : q * w % LANES + w, :]

    press = pa if SWEEPS % 2 == 0 else pb
    for t in range(tiles):
        fields_out[0, t] = eta[t, own : own + tile_x, :]
        for k in range(LAYERS):
            fields_out[1 + k, t] = press[k, t, own : own + tile_x, :]


def turn_kernel(fields, eta_out, press_out):
    for i in range(fields.shape[1]):
        rows = slice(i * LANES, (i + 1) * LANES)
        eta_out[rows, :] = fields[0, i].T
        for k in range(LAYERS):
            press_out[k, rows, :] = fields[1 + k, i].T


def place_load_kernel(n, where_ref, *refs):
    parts, out = refs[:n], refs[n]
    g = where_ref[0]
    tile_x = parts[0].shape[1]
    for shift in range(n):
        col = pl.multiple_of(lax.rem(g - shift + n, n) * tile_x, LANES)
        out[:, pl.ds(col, tile_x)] = parts[shift][...]


def shards(
    slide_thickness,
    footprint,
    slide_momentum,
    bed_friction,
    surface,
    flux_x,
    flux_y,
    bathy_class,
    depth_table,
):
    th, fp, mo, fr = (v[0, 0] for v in (slide_thickness, footprint, slide_momentum, bed_friction))
    w, cells_x = th.shape
    tile_y, tile_x = surface.shape
    n = lax.axis_size("gx")
    secs, gys = lax.axis_size("sec"), lax.axis_size("gy")
    nb = secs * gys
    along = ("sec", "gy")
    g = lax.axis_index("gx")
    b = lax.axis_index(along)
    where = jnp.stack([g, b, jnp.int32(n), jnp.int32(nb)]).astype(jnp.int32)
    deep = tile_x + 2 * RIM
    tiles = tile_y // LANES + 1
    total = TOP + deep + TOP

    def padded(v):
        return v if w >= LANES else jnp.pad(v, ((0, LANES - w), (0, 0)))

    def turn(v, axis, count, by):
        return lax.ppermute(v, axis, [(i, (i + by) % count) for i in range(count)])

    blocks = call(
        functools.partial(pack_slide_kernel, n, tile_x),
        [where],
        [padded(v) for v in (th, fp, mo, fr)],
        [(3 * deep, LANES)] * n,
        [pltpu.VMEM((3, cells_x + 2 * RIM, LANES), F32)],
        name="pack_slide",
    )
    blocks = [blocks[0]] + [turn(blocks[s], "gx", n, s) for s in range(1, n)]

    edge_rows = 6 * EDGE + 8
    low, high, wide, edge_u = call(
        pack_wave_kernel,
        [depth_table],
        [surface, flux_x, flux_y, bathy_class],
        [(edge_rows, tile_x)] * 2 + [(5, tile_x, tile_y), (8, tile_y)],
        [pltpu.VMEM((LAYERS, tile_y + 16, tile_x), F32)],
        name="pack_wave",
    )
    from_low = turn(high, along, nb, 1)
    from_high = turn(low, along, nb, -1)
    halo = (tiles * (5 * RIM + 4), LANES)
    wide, edge_u, send_a, send_b = call(
        widen_wave_kernel,
        [where],
        [wide, edge_u, low, high, from_low, from_high],
        [(5, tiles, tile_x, LANES), (tiles, 8, LANES)] + [halo] * 2,
        name="widen_wave",
    )

    def swap(v, first):
        pairs = [(i, i + 1) for i in range(first, n - 1, 2)]
        return lax.ppermute(v, "gx", pairs + [(j, i) for i, j in pairs])

    got_a = swap(send_a, 0)
    got_b = swap(send_b, 1)

    part = -(-3 * deep // (8 * (LANES // EDGE))) * 8
    rows = part * (LANES // EDGE)
    slide_low, slide_high = call(
        functools.partial(slide_edge_kernel, n, w),
        [where],
        blocks,
        [(part, LANES)] * 2,
        [pltpu.VMEM((rows, LANES), F32)] * 2,
        name="slide_edge",
    )
    slide_from_low = turn(slide_high, along, nb, 1)
    slide_from_high = turn(slide_low, along, nb, -1)

    last_h, last_m = call(
        slide_kernel,
        [],
        [padded(v) for v in (th, fp, mo, fr)],
        [(cells_x, LANES)] * 2,
        [pltpu.VMEM((LANES, cells_x), F32)] * 2,
        name="slide",
    )
    devices = secs * n * gys
    own_rows = cells_x // devices
    both = jnp.stack([v[:, :w].reshape(devices, own_rows, w) for v in (last_h, last_m)], axis=1)
    both = lax.all_to_all(both, ("sec", "gx", "gy"), split_axis=0, concat_axis=0, tiled=True)
    both = both.reshape(secs, n, gys, 2, own_rows, w)
    both = jnp.transpose(both, (3, 4, 0, 2, 1, 5)).reshape(2, own_rows, -1)

    one = (tiles, total, LANES)
    stage_count = 1 if w == LANES else n
    results = call(
        functools.partial(wave_kernel, n, w, cells_x, nb * tile_y),
        [where],
        [wide, edge_u, got_a, got_b, slide_from_low, slide_from_high, *blocks],
        [(w, tile_x)] * n + [(4, tiles - 1, tile_x, LANES)],
        [
            pltpu.VMEM(shape, F32)
            for shape in (
                one,
                (LAYERS, *one),
                (LAYERS, *one),
                (LAYERS, *one),
                (LAYERS, *one),
                (5, *one),
                one,
                (2, *one),
                (2, *one),
                one,
                one,
                one,
                (tiles - 1, total, LANES),
                (stage_count, rows, LANES),
                halo,
                halo,
            )
        ],
        flops=10**9,
        moved=10**7,
        name="wave",
    )
    loads, fields = results[:n], results[n]
    parts = [loads[0]] + [turn(loads[s], "gx", n, s) for s in range(1, n)]
    surface_out, pressure_out = call(
        turn_kernel, [], [fields], [(tile_y, tile_x), (LAYERS, tile_y, tile_x)], name="turn"
    )
    (bottom,) = call(
        functools.partial(place_load_kernel, n), [where], parts, [(w, cells_x)], name="place_load"
    )
    return (surface_out, pressure_out, bottom[None, None], both[0], both[1])


def solution(mesh):
    strip = P(("sec", "gy"), "gx", None, None)
    tile = P(("sec", "gy"), "gx")
    layered = P(None, ("sec", "gy"), "gx")
    return jax.shard_map(
        shards,
        mesh=mesh,
        in_specs=(strip, strip, strip, strip, tile, layered, layered, tile, P()),
        out_specs=(
            tile,
            layered,
            strip,
            P(("sec", "gx", "gy"), None),
            P(("sec", "gx", "gy"), None),
        ),
        check_vma=False,
    )
```

profile of v0, /device:TPU:0, one launch (start us, length us, event | category | flops | bytes accessed | tf_op | source)
XLA Modules:
  0.0 115.9 jit_solution(17075551883917940376)
XLA Ops:
  0.6 8.0 %slide.1 = (f32[512,128]{1,0:T(8,128)}, f32[512,128]{1,0:T(8,128)}) custom-call(f32[128,512]{1,0:T(8,128)} %bitcast.17, s32[128,512]{1,0:T(8,128)} %bitcast.19, f32[128,512]{1,0:T(8,128)} %bitcast.21, f32[128,512]{1,0:T(8,128)} %bitcast.23), custom_call_target="tpu_custom_call" | custom-call | flops 1000000 | bytes 1000000 | tf_op jit(solution)/shard_map/slide/pallas_call | solution.py:39
  8.6 1.9 %pad_maximum_fusion = f32[32,2,16,128]{3,2,1,0:T(8,128)} fusion(f32[32,1,16,128]{3,2,1,0:T(8,128)} %bitcast.27, f32[32,1,16,128]{3,2,1,0:T(8,128)} %bitcast.26), kind=kLoop, calls=%fused_computation | loop fusion | flops 131072 | bytes 1048576 | tf_op jit(solution)/shard_map/stack | solution.py:629
  10.4 7.3 %all-to-all-start = ((f32[32,2,16,128]{3,2,1,0:T(8,128)}), f32[32,2,16,128]{3,2,1,0:T(8,128)S(1)}, u32[]{:S(2)}, u32[]{:S(2)}) async-start(f32[32,2,16,128]{3,2,1,0:T(8,128)} %pad_maximum_fusion), calls=%async_computation | async-start | bytes 1048576 | tf_op jit(solution)/shard_map/all_to_all | solution.py:630
  17.8 3.8 %pack_wave.1 = (f32[200,128]{1,0:T(8,128)}, f32[200,128]{1,0:T(8,128)}, f32[5,128,512]{2,1,0:T(8,128)}, f32[8,512]{1,0:T(8,128)}) custom-call(f32[8]{0:T(128)} %table.1, f32[512,128]{1,0:T(8,128)} %eta.1, f32[3,512,128]{2,1,0:T(8,128)} %fx.1, f32[3,512,128]{2,1,0:T(8,128)} %fy.1, s32[512,128]{1,0:T(8,128)} %cls.1), custom_call_target="tpu_custom_call" | custom-call | flops 1000000 | bytes 1000000 | tf_op jit(solution)/shard_map/pack_wave/pallas_call | solution.py:39
  21.5 1.8 %collective-permute-start = (f32[200,128]{1,0:T(8,128)}, f32[200,128]{1,0:T(8,128)S(1)}, u32[]{:S(2)}, u32[]{:S(2)}) collective-permute-start(f32[200,128]{1,0:T(8,128)} %get-tuple-element.31.high), channel_id=1, source_target_pairs={{0,1},{1,2},{2,3},{3,16},{16,17},{17,18},{18,19},{19,0},{4,5},{5,6... | collective-permute-start | bytes 307208 | tf_op jit(solution)/shard_map/ppermute | solution.py:567
  23.3 0.9 collective-permute-start.1
  24.2 0.6 pad_add_fusion.where_ref
  24.8 3.7 %collective-permute-done.from_low = f32[200,128]{1,0:T(8,128)S(1)} collective-permute-done((f32[200,128]{1,0:T(8,128)}, f32[200,128]{1,0:T(8,128)S(1)}, u32[]{:S(2)}, u32[]{:S(2)}) %collective-permute-start) | collective-permute-done | bytes 102432 | tf_op jit(solution)/shard_map/ppermute | solution.py:567
  28.4 3.7 %collective-permute-done.1.from_high = f32[200,128]{1,0:T(8,128)S(1)} collective-permute-done((f32[200,128]{1,0:T(8,128)}, f32[200,128]{1,0:T(8,128)S(1)}, u32[]{:S(2)}, u32[]{:S(2)}) %collective-permute-start.1) | collective-permute-done | bytes 102432 | tf_op jit(solution)/shard_map/ppermute | solution.py:567
  32.2 0.6 copy-done.4
  32.8 3.1 %widen_wave.1 = (f32[5,5,128,128]{3,2,1,0:T(8,128)}, f32[5,8,128]{2,1,0:T(8,128)}, f32[720,128]{1,0:T(8,128)}, f32[720,128]{1,0:T(8,128)}) custom-call(s32[4]{0:T(128)} %pad_add_fusion.where_ref, f32[5,128,512]{2,1,0:T(8,128)} %get-tuple-element.28.wide, f32[8,512]{1,0:T(8,128)} %get-tuple-element.29.edge_u, f32[200,128]{1,0:T(8,128)} %get-tuple-element.30.low, ...), custom_call_target="tpu_custom_call" | custom-call | flops 1000000 | bytes 1000000 | tf_op jit(solution)/shard_map/widen_wave/pallas_call | solution.py:39
  35.9 1.9 %collective-permute-start.2 = (f32[720,128]{1,0:T(8,128)}, f32[720,128]{1,0:T(8,128)S(1)}, u32[]{:S(2)}, u32[]{:S(2)}) collective-permute-start(f32[720,128]{1,0:T(8,128)} %get-tuple-element.34), channel_id=1, source_target_pairs={{0,4},{8,12},{4,0},{12,8},{1,5},{9,13},{5,1},{13,9},{2,6},{10,14},... | collective-permute-start | bytes 1105928 | tf_op jit(solution)/shard_map/ppermute | solution.py:601
  37.8 0.7 collective-permute-start.3
  38.5 2.6 %pack_slide.1 = (f32[552,128]{1,0:T(8,128)}, f32[552,128]{1,0:T(8,128)}, f32[552,128]{1,0:T(8,128)}, f32[552,128]{1,0:T(8,128)}) custom-call(s32[4]{0:T(128)} %pad_add_fusion.where_ref, f32[128,512]{1,0:T(8,128)} %bitcast.18, s32[128,512]{1,0:T(8,128)} %bitcast.20, f32[128,512]{1,0:T(8,128)} %bitcast.22, f32[128,512]{1,0:T(8,128)} %bitcast.24), custom_call_target="tpu_custom_call" | custom-call | flops 1000000 | bytes 1000000 | tf_op jit(solution)/shard_map/pack_slide/pallas_call | solution.py:39
  41.1 3.7 %collective-permute-start.4 = (f32[552,128]{1,0:T(8,128)}, f32[552,128]{1,0:T(8,128)S(1)}, u32[]{:S(2)}, u32[]{:S(2)}) collective-permute-start(f32[552,128]{1,0:T(8,128)} %get-tuple-element.37), channel_id=1, source_target_pairs={{0,4},{4,8},{8,12},{12,0},{1,5},{5,9},{9,13},{13,1},{2,6},{6,10},{... | collective-permute-start | bytes 847880 | tf_op jit(solution)/shard_map/ppermute | solution.py:567
  44.9 0.0 collective-permute-start.5
  44.9 2.4 %collective-permute-start.6 = (f32[552,128]{1,0:T(8,128)}, f32[552,128]{1,0:T(8,128)S(1)}, u32[]{:S(2)}, u32[]{:S(2)}) collective-permute-start(f32[552,128]{1,0:T(8,128)} %get-tuple-element.39), channel_id=1, source_target_pairs={{0,12},{4,0},{8,4},{12,8},{1,13},{5,1},{9,5},{13,9},{2,14},{6,2},{... | collective-permute-start | bytes 847880 | tf_op jit(solution)/shard_map/ppermute | solution.py:567
  47.2 8.2 %collective-permute-done.4.refs_1_.refs_7_ = f32[552,128]{1,0:T(8,128)S(1)} collective-permute-done((f32[552,128]{1,0:T(8,128)}, f32[552,128]{1,0:T(8,128)S(1)}, u32[]{:S(2)}, u32[]{:S(2)}) %collective-permute-start.4) | collective-permute-done | bytes 282656 | tf_op jit(solution)/shard_map/ppermute | solution.py:567
  55.4 14.1 %collective-permute-done.5.refs_2_.refs_8_ = f32[552,128]{1,0:T(8,128)S(1)} collective-permute-done((f32[552,128]{1,0:T(8,128)}, f32[552,128]{1,0:T(8,128)S(1)}, u32[]{:S(2)}, u32[]{:S(2)}) %collective-permute-start.5) | collective-permute-done | bytes 282656 | tf_op jit(solution)/shard_map/ppermute | solution.py:567
  69.5 0.0 collective-permute-done.6.refs_3_.refs_9_
  69.5 0.7 copy-done.1
  70.2 0.1 copy-done.2
  70.3 2.1 %slide_edge.1 = (f32[144,128]{1,0:T(8,128)}, f32[144,128]{1,0:T(8,128)}) custom-call(s32[4]{0:T(128)} %pad_add_fusion.where_ref, f32[552,128]{1,0:T(8,128)} %get-tuple-element.36.refs_0_.refs_6_, f32[552,128]{1,0:T(8,128)} %copy-done, f32[552,128]{1,0:T(8,128)} %copy-done.1, f32[552,128]{1,0:T(8,128)} %copy-done.2), custom_call_target="tpu_custom_call" | custom-call | flops 1000000 | bytes 1000000 | tf_op jit(solution)/shard_map/slide_edge/pallas_call | solution.py:39
  72.4 1.3 %collective-permute-start.7 = (f32[144,128]{1,0:T(8,128)}, f32[144,128]{1,0:T(8,128)S(1)}, u32[]{:S(2)}, u32[]{:S(2)}) collective-permute-start(f32[144,128]{1,0:T(8,128)} %get-tuple-element.40), channel_id=1, source_target_pairs={{0,1},{1,2},{2,3},{3,16},{16,17},{17,18},{18,19},{19,0},{4,5},{5,6... | collective-permute-start | bytes 221192 | tf_op jit(solution)/shard_map/ppermute | solution.py:567
  73.7 1.4 %collective-permute-start.8 = (f32[144,128]{1,0:T(8,128)}, f32[144,128]{1,0:T(8,128)S(1)}, u32[]{:S(2)}, u32[]{:S(2)}) collective-permute-start(f32[144,128]{1,0:T(8,128)} %get-tuple-element.41), channel_id=1, source_target_pairs={{0,19},{1,0},{2,1},{3,2},{16,3},{17,16},{18,17},{19,18},{4,23},{5,... | collective-permute-start | bytes 221192 | tf_op jit(solution)/shard_map/ppermute | solution.py:567
  75.1 2.2 %collective-permute-done.7.refs_4_ = f32[144,128]{1,0:T(8,128)S(1)} collective-permute-done((f32[144,128]{1,0:T(8,128)}, f32[144,128]{1,0:T(8,128)S(1)}, u32[]{:S(2)}, u32[]{:S(2)}) %collective-permute-start.7) | collective-permute-done | bytes 73760 | tf_op jit(solution)/shard_map/ppermute | solution.py:567
  77.3 1.0 collective-permute-done.8.refs_5_
  78.3 0.0 collective-permute-done.2.refs_2_
  78.3 0.0 collective-permute-done.3.refs_3_
  78.3 0.6 copy-done.11
  78.9 0.1 copy-done.8
  79.0 0.1 copy-done.9
  79.1 19.9 %wave.1 = (f32[128,128]{1,0:T(8,128)}, f32[128,128]{1,0:T(8,128)}, f32[128,128]{1,0:T(8,128)}, f32[128,128]{1,0:T(8,128)}, f32[4,4,128,128]{3,2,1,0:T(8,128)}) custom-call(s32[4]{0:T(128)} %pad_add_fusion.where_ref, f32[5,5,128,128]{3,2,1,0:T(8,128)} %get-tuple-element.32.refs_0_, f32[5,8,128]{2,1,0:T(8,128)} %get-tuple-element.33.refs_1_, ...), custom_call_target="tpu_custom_call" | custom-call | flops 1000000000 | bytes 10000000 | tf_op jit(solution)/shard_map/wave/pallas_call | solution.py:39
  99.0 5.1 %collective-permute-start.9 = (f32[128,128]{1,0:T(8,128)}, f32[128,128]{1,0:T(8,128)S(1)}, u32[]{:S(2)}, u32[]{:S(2)}) collective-permute-start(f32[128,128]{1,0:T(8,128)} %get-tuple-element.46), channel_id=1, source_target_pairs={{0,4},{4,8},{8,12},{12,0},{1,5},{5,9},{9,13},{13,1},{2,6},{6,10},{... | collective-permute-start | bytes 196616 | tf_op jit(solution)/shard_map/ppermute | solution.py:567
  104.1 2.7 %collective-permute-start.10 = (f32[128,128]{1,0:T(8,128)}, f32[128,128]{1,0:T(8,128)S(1)}, u32[]{:S(2)}, u32[]{:S(2)}) collective-permute-start(f32[128,128]{1,0:T(8,128)} %get-tuple-element.47), channel_id=1, source_target_pairs={{0,8},{4,12},{8,0},{12,4},{1,9},{5,13},{9,1},{13,5},{2,10},{6,14},... | collective-permute-start | bytes 196616 | tf_op jit(solution)/shard_map/ppermute | solution.py:567
  106.9 0.0 collective-permute-start.11
  106.9 2.5 %turn.1 = (f32[512,128]{1,0:T(8,128)}, f32[3,512,128]{2,1,0:T(8,128)}) custom-call(f32[4,4,128,128]{3,2,1,0:T(8,128)} %get-tuple-element.42.fields), custom_call_target="tpu_custom_call" | custom-call | flops 1000000 | bytes 1000000 | tf_op jit(solution)/shard_map/turn/pallas_call | solution.py:39
  109.4 0.0 collective-permute-done.9.refs_1_
  109.4 1.8 %collective-permute-done.10.refs_2_ = f32[128,128]{1,0:T(8,128)S(1)} collective-permute-done((f32[128,128]{1,0:T(8,128)}, f32[128,128]{1,0:T(8,128)S(1)}, u32[]{:S(2)}, u32[]{:S(2)}) %collective-permute-start.10) | collective-permute-done | bytes 65568 | tf_op jit(solution)/shard_map/ppermute | solution.py:567
  111.2 0.4 collective-permute-done.11.refs_3_
  111.6 0.2 copy-done.6
  111.9 0.4 copy-done.7
  112.2 1.7 %place_load.1 = f32[128,512]{1,0:T(8,128)} custom-call(s32[4]{0:T(128)} %pad_add_fusion.where_ref, f32[128,128]{1,0:T(8,128)} %get-tuple-element.45.refs_0_, f32[128,128]{1,0:T(8,128)} %copy-done.5, f32[128,128]{1,0:T(8,128)} %copy-done.6, f32[128,128]{1,0:T(8,128)} %copy-done.7), custom_call_target="tpu_custom_call" | custom-call | flops 1000000 | bytes 1000000 | tf_op jit(solution)/shard_map/place_load/pallas_call | solution.py:39
  113.9 0.0 all-to-all-done
  114.0 0.2 copy.17
  114.1 0.8 squeeze.22
  115.0 0.2 copy.18
  115.1 0.8 squeeze.23
  (17 shorter events, 0.1 us)
Async XLA Ops:
  10.4 103.5 %all-to-all-start = ((f32[32,2,16,128]{3,2,1,0:T(8,128)}), f32[32,2,16,128]{3,2,1,0:T(8,128)S(1)}, u32[]{:S(2)}, u32[]{:S(2)}) async-start(f32[32,2,16,128]{3,2,1,0:T(8,128)} %pad_maximum_fusion), calls=%async_computation | async-start | bytes 1048576 | tf_op jit(solution)/shard_map/all_to_all | solution.py:630
  21.5 6.9 %collective-permute-start = (f32[200,128]{1,0:T(8,128)}, f32[200,128]{1,0:T(8,128)S(1)}, u32[]{:S(2)}, u32[]{:S(2)}) collective-permute-start(f32[200,128]{1,0:T(8,128)} %get-tuple-element.31.high), channel_id=1, source_target_pairs={{0,1},{1,2},{2,3},{3,16},{16,17},{17,18},{18,19},{19,0},{4,5},{5,6... | collective-permute-start | bytes 307208 | tf_op jit(solution)/shard_map/ppermute | solution.py:567
  23.3 8.9 %collective-permute-start.1 = (f32[200,128]{1,0:T(8,128)}, f32[200,128]{1,0:T(8,128)S(1)}, u32[]{:S(2)}, u32[]{:S(2)}) collective-permute-start(f32[200,128]{1,0:T(8,128)} %get-tuple-element.30.low), channel_id=1, source_target_pairs={{0,19},{1,0},{2,1},{3,2},{16,3},{17,16},{18,17},{19,18},{4,23},{5,... | collective-permute-start | bytes 307208 | tf_op jit(solution)/shard_map/ppermute | solution.py:567
  28.4 3.7 %copy-start.3 = (f32[200,128]{1,0:T(8,128)}, f32[200,128]{1,0:T(8,128)S(1)}, u32[]{:S(2)}) copy-start(f32[200,128]{1,0:T(8,128)S(1)} %collective-permute-done.from_low) | copy-start | bytes 307204
  32.2 0.6 copy-start.4
  35.9 42.3 %collective-permute-start.2 = (f32[720,128]{1,0:T(8,128)}, f32[720,128]{1,0:T(8,128)S(1)}, u32[]{:S(2)}, u32[]{:S(2)}) collective-permute-start(f32[720,128]{1,0:T(8,128)} %get-tuple-element.34), channel_id=1, source_target_pairs={{0,4},{8,12},{4,0},{12,8},{1,5},{9,13},{5,1},{13,9},{2,6},{10,14},... | collective-permute-start | bytes 1105928 | tf_op jit(solution)/shard_map/ppermute | solution.py:601
  37.8 40.4 %collective-permute-start.3 = (f32[720,128]{1,0:T(8,128)}, f32[720,128]{1,0:T(8,128)S(1)}, u32[]{:S(2)}, u32[]{:S(2)}) collective-permute-start(f32[720,128]{1,0:T(8,128)} %get-tuple-element.35), channel_id=1, source_target_pairs={{4,8},{8,4},{5,9},{9,5},{6,10},{10,6},{7,11},{11,7},{20,24},{24,20... | collective-permute-start | bytes 1105928 | tf_op jit(solution)/shard_map/ppermute | solution.py:601
  41.1 14.3 %collective-permute-start.4 = (f32[552,128]{1,0:T(8,128)}, f32[552,128]{1,0:T(8,128)S(1)}, u32[]{:S(2)}, u32[]{:S(2)}) collective-permute-start(f32[552,128]{1,0:T(8,128)} %get-tuple-element.37), channel_id=1, source_target_pairs={{0,4},{4,8},{8,12},{12,0},{1,5},{5,9},{9,13},{13,1},{2,6},{6,10},{... | collective-permute-start | bytes 847880 | tf_op jit(solution)/shard_map/ppermute | solution.py:567
  44.9 24.6 %collective-permute-start.5 = (f32[552,128]{1,0:T(8,128)}, f32[552,128]{1,0:T(8,128)S(1)}, u32[]{:S(2)}, u32[]{:S(2)}) collective-permute-start(f32[552,128]{1,0:T(8,128)} %get-tuple-element.38), channel_id=1, source_target_pairs={{0,8},{4,12},{8,0},{12,4},{1,9},{5,13},{9,1},{13,5},{2,10},{6,14},... | collective-permute-start | bytes 847880 | tf_op jit(solution)/shard_map/ppermute | solution.py:567
  44.9 24.6 %collective-permute-start.6 = (f32[552,128]{1,0:T(8,128)}, f32[552,128]{1,0:T(8,128)S(1)}, u32[]{:S(2)}, u32[]{:S(2)}) collective-permute-start(f32[552,128]{1,0:T(8,128)} %get-tuple-element.39), channel_id=1, source_target_pairs={{0,12},{4,0},{8,4},{12,8},{1,13},{5,1},{9,5},{13,9},{2,14},{6,2},{... | collective-permute-start | bytes 847880 | tf_op jit(solution)/shard_map/ppermute | solution.py:567
  55.4 14.1 %copy-start = (f32[552,128]{1,0:T(8,128)}, f32[552,128]{1,0:T(8,128)S(1)}, u32[]{:S(2)}) copy-start(f32[552,128]{1,0:T(8,128)S(1)} %collective-permute-done.4.refs_1_.refs_7_) | copy-start | bytes 847876
  69.5 0.7 copy-start.1
  69.5 0.8 copy-start.2
  72.4 4.9 %collective-permute-start.7 = (f32[144,128]{1,0:T(8,128)}, f32[144,128]{1,0:T(8,128)S(1)}, u32[]{:S(2)}, u32[]{:S(2)}) collective-permute-start(f32[144,128]{1,0:T(8,128)} %get-tuple-element.40), channel_id=1, source_target_pairs={{0,1},{1,2},{2,3},{3,16},{16,17},{17,18},{18,19},{19,0},{4,5},{5,6... | collective-permute-start | bytes 221192 | tf_op jit(solution)/shard_map/ppermute | solution.py:567
  73.7 4.6 %collective-permute-start.8 = (f32[144,128]{1,0:T(8,128)}, f32[144,128]{1,0:T(8,128)S(1)}, u32[]{:S(2)}, u32[]{:S(2)}) collective-permute-start(f32[144,128]{1,0:T(8,128)} %get-tuple-element.41), channel_id=1, source_target_pairs={{0,19},{1,0},{2,1},{3,2},{16,3},{17,16},{18,17},{19,18},{4,23},{5,... | collective-permute-start | bytes 221192 | tf_op jit(solution)/shard_map/ppermute | solution.py:567
  77.3 1.0 copy-start.10
  78.3 0.6 copy-start.11
  78.3 0.8 copy-start.8
  78.3 0.9 copy-start.9
  99.0 10.4 %collective-permute-start.9 = (f32[128,128]{1,0:T(8,128)}, f32[128,128]{1,0:T(8,128)S(1)}, u32[]{:S(2)}, u32[]{:S(2)}) collective-permute-start(f32[128,128]{1,0:T(8,128)} %get-tuple-element.46), channel_id=1, source_target_pairs={{0,4},{4,8},{8,12},{12,0},{1,5},{5,9},{9,13},{13,1},{2,6},{6,10},{... | collective-permute-start | bytes 196616 | tf_op jit(solution)/shard_map/ppermute | solution.py:567
  104.1 7.1 %collective-permute-start.10 = (f32[128,128]{1,0:T(8,128)}, f32[128,128]{1,0:T(8,128)S(1)}, u32[]{:S(2)}, u32[]{:S(2)}) collective-permute-start(f32[128,128]{1,0:T(8,128)} %get-tuple-element.47), channel_id=1, source_target_pairs={{0,8},{4,12},{8,0},{12,4},{1,9},{5,13},{9,1},{13,5},{2,10},{6,14},... | collective-permute-start | bytes 196616 | tf_op jit(solution)/shard_map/ppermute | solution.py:567
  106.9 4.7 %collective-permute-start.11 = (f32[128,128]{1,0:T(8,128)}, f32[128,128]{1,0:T(8,128)S(1)}, u32[]{:S(2)}, u32[]{:S(2)}) collective-permute-start(f32[128,128]{1,0:T(8,128)} %get-tuple-element.48), channel_id=1, source_target_pairs={{0,12},{4,0},{8,4},{12,8},{1,13},{5,1},{9,5},{13,9},{2,14},{6,2},{... | collective-permute-start | bytes 196616 | tf_op jit(solution)/shard_map/ppermute | solution.py:567
  109.4 2.2 %copy-start.5 = (f32[128,128]{1,0:T(8,128)}, f32[128,128]{1,0:T(8,128)S(1)}, u32[]{:S(2)}) copy-start(f32[128,128]{1,0:T(8,128)S(1)} %collective-permute-done.9.refs_1_) | copy-start | bytes 196612
  111.2 0.6 copy-start.6
  111.6 0.6 copy-start.7
where the time goes:
time: 116 us
  Pallas kernels  43.6 us (38%)
  waiting for transfers between devices  35.1 us (30%)
  starting transfers between devices  29.1 us (25%)
  local copies, waits for them, and re-layouts  4.93 us (4%)
  other arithmetic  2.45 us (2%)
    pallas_call x8, Pallas kernels, call(): pl.pallas_call(kernel, out_shape=[jax.ShapeDtypeStruct(s, F32) for s in o...  43.6 us
    ppermute x10, waiting for transfers between devices, turn(): return lax.ppermute(v, axis, [(i, (i + by) % count) for i in range(count)])  35.1 us
    ppermute x10, starting transfers between devices, turn(): return lax.ppermute(v, axis, [(i, (i + by) % count) for i in range(count)])  19.3 us
    all_to_all x1, starting transfers between devices, shards(): lax.all_to_all(both, ('sec', 'gx', 'gy'), split_axis=0, concat_axis=0, ti...  7.33 us
    unnamed x24, local copies, waits for them, and re-layouts  2.93 us
    ppermute x2, starting transfers between devices, swap(): return lax.ppermute(v, 'gx', pairs + [(j, i) for i, j in pairs])  2.56 us
  transfers between devices with their start and end apart: 13, of which 8 were waited for; matrix products, arithmetic and copies ran while one was open for 1% of the time, Pallas kernels for 31%

commit v1 on v0

--- a/solution.py
+++ b/solution.py
@@ -6,6 +6,7 @@
 from jax.experimental import pallas as pl
 from jax.experimental.pallas import tpu as pltpu
 from jax.sharding import PartitionSpec as P
+
 
 LEVELS = 4
 SWEEPS = 4
@@ -21,8 +22,10 @@
 
 STEP = SWEEPS + 3
 RIM = LEVELS * STEP
+TRIM = STEP + 1
 EDGE = 32
 LANES = 128
+GROUP = 2
 TOP = 8
 F32 = jnp.float32
 
@@ -35,16 +38,55 @@
     return pl.BlockSpec(memory_space=pltpu.VMEM)
 
 
-def call(kernel, scalars, inputs, outs, scratch=(), flops=10**6, moved=10**6, name=None):
+def fetching(kernel, lead, count):
+    def body(*refs):
+        scalars, inputs, rest = refs[:lead], refs[lead : lead + count], refs[lead + count :]
+        held, sems = rest[-count - 1 : -1], rest[-1]
+        copies = [
+            pltpu.make_async_copy(src, dst, sems.at[i])
+            for i, (src, dst) in enumerate(zip(inputs, held))
+        ]
+        for copy in copies:
+            copy.start()
+        for copy in copies:
+            copy.wait()
+        kernel(*scalars, *held, *rest[: -count - 1])
+
+    return body
+
+
+def call(kernel, scalars, inputs, outs, scratch=(), flops=10**6, moved=10**6, room=12, fetch=False):
+    in_spec, scratch = vmem(), list(scratch)
+    if fetch:
+        in_spec = pl.BlockSpec(memory_space=pltpu.HBM)
+        kernel = fetching(kernel, len(scalars), len(inputs))
+        scratch += [pltpu.VMEM(v.shape, v.dtype) for v in inputs]
+        scratch.append(pltpu.SemaphoreType.DMA((len(inputs),)))
     return pl.pallas_call(
         kernel,
         out_shape=[jax.ShapeDtypeStruct(s, F32) for s in outs],
-        in_specs=[smem()] * len(scalars) + [vmem()] * len(inputs),
+        in_specs=[smem()] * len(scalars) + [in_spec] * len(inputs),
         out_specs=[vmem() for _ in outs],
-        scratch_shapes=list(scratch),
+        scratch_shapes=scratch,
         cost_estimate=pl.CostEstimate(flops=flops, bytes_accessed=moved, transcendentals=0),
-        name=name,
+        compiler_params=pltpu.CompilerParams(vmem_limit_bytes=room << 20),
     )(*scalars, *inputs)
+
+
+def strip_place():
+    return lax.axis_index("gx")
+
+
+def band_place():
+    return lax.axis_index("sec") * lax.axis_size("gy") + lax.axis_index("gy")
+
+
+def receiver(g, shift, n):
+    return lax.bitwise_xor(g, shift) if n & (n - 1) == 0 else lax.rem(g + shift, n)
+
+
+def sender(g, shift, n):
+    return lax.bitwise_xor(g, shift) if n & (n - 1) == 0 else lax.rem(g - shift + n, n)
 
 
 def lane_of(shape):
@@ -55,11 +97,11 @@
     return lax.broadcasted_iota(jnp.int32, shape, len(shape) - 2)
 
 
-def pack_slide_kernel(n, tile_x, where_ref, th, fp, mo, fr, *rest):
+def pack_slide_kernel(n, tile_x, th, fp, mo, fr, *rest):
     blocks, turned = rest[:n], rest[n]
     cells_x = th.shape[1]
     deep = tile_x + 2 * RIM
-    g = where_ref[0]
+    g = strip_place()
     fields = (
         lambda cols: th[:, cols] * fp[:, cols].astype(F32),
         lambda cols: mo[:, cols],
@@ -73,48 +115,60 @@
                 slice(i * LANES, (i + 1) * LANES)
             ).T
     for shift in range(n):
-        start = pl.multiple_of(lax.rem(g + shift, n) * tile_x, 8)
+        start = pl.multiple_of(receiver(g, shift, n) * tile_x, 8)
         for a in range(3):
-            blocks[shift][a * deep : (a + 1) * deep, :] = turned[a, pl.ds(start, deep), :]
-
-
-def slide_kernel(th, fp, mo, fr, out_h, out_m, hs, ms):
-    w, cells = th.shape
-    lane = lane_of((8, cells))
-
-    def body(c, carry):
-        rows = pl.ds(pl.multiple_of(c * 8, 8), 8)
-        h = th[rows, :] * fp[rows, :].astype(F32)
-        m = mo[rows, :]
-        f = fr[rows, :]
-
-        def lo(v):
-            return jnp.where(lane == 0, 0.0, pltpu.roll(v, 1, 1))
-
-        def hi(v):
-            return jnp.where(lane == cells - 1, 0.0, pltpu.roll(v, cells - 1, 1))
-
-        for _ in range(LEVELS):
-            u = m / (1.0 + jnp.abs(h))
-            carry_m = m * u + 0.5 * h * h
-            drag = f * h * u / jnp.sqrt(u * u + 1.0)
-            m_lo, m_hi = lo(m), hi(m)
-            new_h = 0.5 * (lo(h) + hi(h)) - 0.5 * COURANT * (m_hi - m_lo)
-            m = (
-                0.5 * (m_lo + m_hi)
-                - 0.5 * COURANT * (hi(carry_m) - lo(carry_m))
-                + COURANT * (SLOPE_PULL * h - drag)
-            )
-            h = new_h
-        hs[rows, :] = h
-        ms[rows, :] = m
-        return carry
-
-    lax.fori_loop(0, w // 8, body, 0)
+            cut = TRIM if a == 2 else 0
+            size = deep - 2 * cut
+            blocks[shift][a * deep : a * deep + size, :] = turned[a, pl.ds(start + cut, size), :]
+
+
+def slide_kernel(th, fp, mo, fr, out, hs, ms, qs, fs):
+    devices, _, own_rows, _ = out.shape
+    cells = th.shape[1]
+    zero = jnp.zeros((8, LANES), F32)
+    for ref in (hs.at[0], hs.at[1], ms.at[0], ms.at[1], qs):
+        ref[:8, :] = zero
+        ref[8 + cells :, :] = zero
     for i in range(cells // LANES):
         cols = slice(i * LANES, (i + 1) * LANES)
-        out_h[cols, :] = hs[:, cols].T
-        out_m[cols, :] = ms[:, cols].T
+        at = slice(8 + i * LANES, 8 + (i + 1) * LANES)
+        hs[0, at, :] = (th[:, cols] * fp[:, cols].astype(F32)).T
+        ms[0, at, :] = mo[:, cols].T
+        fs[at, :] = fr[:, cols].T
+    rows = 32 if cells % 32 == 0 else 8
+    for level in range(LEVELS):
+        h_now, h_new = hs.at[level % 2], hs.at[(level + 1) % 2]
+        m_now, m_new = ms.at[level % 2], ms.at[(level + 1) % 2]
+        for c in range(cells // rows):
+            at = slice(8 + c * rows, 8 + (c + 1) * rows)
+            h, m = h_now[at, :], m_now[at, :]
+            u = m / (1.0 + jnp.abs(h))
+            qs[at, :] = m * u + 0.5 * h * h
+            m_new[at, :] = COURANT * (SLOPE_PULL * h - fs[at, :] * h * u * lax.rsqrt(u * u + 1.0))
+        for c in range(cells // rows):
+            at = slice(8 + c * rows, 8 + (c + 1) * rows)
+            lo = slice(7 + c * rows, 7 + (c + 1) * rows)
+            hi = slice(9 + c * rows, 9 + (c + 1) * rows)
+            m_lo, m_hi = m_now[lo, :], m_now[hi, :]
+            h_new[at, :] = 0.5 * (h_now[lo, :] + h_now[hi, :]) - 0.5 * COURANT * (m_hi - m_lo)
+            m_new[at, :] = (
+                0.5 * (m_lo + m_hi) - 0.5 * COURANT * (qs[hi, :] - qs[lo, :])
+            ) + m_new[at, :]
+    for d in range(devices):
+        at = slice(8 + d * own_rows, 8 + (d + 1) * own_rows)
+        out[d, 0] = hs[LEVELS % 2, at, :]
+        out[d, 1] = ms[LEVELS % 2, at, :]
+
+
+def place_slide_kernel(secs, n, gys, both, out_h, out_m):
+    w = both.shape[3]
+    for s in range(secs):
+        for g in range(n):
+            for y in range(gys):
+                at = ((s * gys + y) * n + g) * w
+                src = (s * n + g) * gys + y
+                out_h[:, at : at + w] = both[src, 0]
+                out_m[:, at : at + w] = both[src, 1]
 
 
 def pack_wave_kernel(table, eta, fx, fy, cls, low, high, wide, edge_u, v_pad):
@@ -129,7 +183,7 @@
     for i in range(tile_y // LANES):
         rows = slice(i * LANES, (i + 1) * LANES)
 
-        def keep(a, value, turned=True):
+        def keep(a, value):
             if i == 0:
                 low[a * EDGE : (a + 1) * EDGE, :] = value[:EDGE]
             if i == last:
@@ -165,8 +219,8 @@
         high[base + k : base + k + 1, :] = fy[k, tile_y - 1 : tile_y, :]
 
 
-def widen_wave_kernel(where_ref, wide, edge_u, low, high, from_low, from_high, out, out_u, send_a, send_b):
-    g, b, nb = where_ref[0], where_ref[1], where_ref[3]
+def widen_wave_kernel(nb, wide, edge_u, low, high, from_low, from_high, out, out_u, send_a, send_b):
+    g, b = strip_place(), band_place()
     tile_x, tile_y = wide.shape[1:]
     tiles = tile_y // LANES
     has_low = (b > 0).astype(F32)
@@ -226,21 +280,21 @@
         fill(send_b, True)
 
 
-def slide_edge_kernel(n, w, where_ref, *refs):
+def slide_edge_kernel(n, w, *refs):
     blocks = refs[:n]
     low, high, head, tail = refs[n:]
-    g = where_ref[0]
+    g = strip_place()
     rows = blocks[0].shape[0]
     part = low.shape[0]
     head[rows:, :] = jnp.zeros((head.shape[0] - rows, LANES), F32)
     tail[rows:, :] = jnp.zeros((tail.shape[0] - rows, LANES), F32)
     for shift in range(n):
 
-        @pl.when(g == shift)
+        @pl.when(sender(g, shift, n) == 0)
         def _():
             head[:rows, :] = blocks[shift][...]
 
-        @pl.when(lax.rem(g + 1, n) == shift)
+        @pl.when(sender(g, shift, n) == n - 1)
         def _():
             tail[:rows, :] = blocks[shift][...]
 
@@ -259,15 +313,15 @@
     high[...] = packed_high
 
 
-def wave_kernel(n, w, cells_x, cells_y, where_ref, *refs):
+def wave_kernel(n, w, cells_x, cells_y, *refs):
     (wide, edge_u, got_a, got_b, slide_low, slide_high) = refs[:6]
     blocks = refs[6 : 6 + n]
     loads = refs[6 + n : 6 + 2 * n]
     fields_out = refs[6 + 2 * n]
-    (eta, div, src, pa, pb, coef, corner, hs, ms, fs, qs, rise, load, stage, left, right) = refs[
+    (eta, div, src, pa, pb, coef, corner, hs, ms, fs, qs, rise, load, bottoms, stage, left, right) = refs[
         7 + 2 * n :
     ]
-    g, b = where_ref[0], where_ref[1]
+    g, b = strip_place(), band_place()
     tiles, tile_x = wide.shape[1] - 1, wide.shape[2]
     every = range(tiles + 1)
     tile_y = tiles * LANES
@@ -314,25 +368,32 @@
             bump(own, -left[base + k : base + k + 1, :])
             bump(own - 1, edge_u[t, k : k + 1, :])
 
-    slides = (hs.at[0], ms.at[0], fs)
+    slides = (
+        (hs.at[0], TOP, 0, deep),
+        (ms.at[0], TOP, deep, deep),
+        (fs, TOP + TRIM, 2 * deep, deep - 2 * TRIM),
+    )
+    for t in every:
+        fs[t, TOP : TOP + TRIM, :] = jnp.zeros((TRIM, LANES), F32)
+        fs[t, TOP + deep - TRIM : TOP + deep, :] = jnp.zeros((TRIM, LANES), F32)
     if w == LANES:
         for shift in range(n):
-            q = lax.rem(g - shift + n, n)
-            for a, ref in enumerate(slides):
-                ref[q, TOP : TOP + deep, :] = blocks[shift][a * deep : (a + 1) * deep, :]
+            q = sender(g, shift, n)
+            for ref, to, at, size in slides:
+                ref[q, to : to + size, :] = blocks[shift][at : at + size, :]
     else:
         per = LANES // w
-        lane_d = lane_of((deep, LANES))
-        for a, ref in enumerate(slides):
+        for ref, to, at, size in slides:
+            lane_d = lane_of((size, LANES))
             for shift in range(n):
-                stage[lax.rem(g - shift + n, n), :deep, :] = blocks[shift][a * deep : (a + 1) * deep, :]
+                stage[sender(g, shift, n), :size, :] = blocks[shift][at : at + size, :]
             for t in range(tiles):
-                v = stage[t * per, :deep, :]
+                v = stage[t * per, :size, :]
                 for j in range(1, per):
                     v = jnp.where(
-                        lane_d < j * w, v, pltpu.roll(stage[t * per + j, :deep, :], j * w, 1)
+                        lane_d < j * w, v, pltpu.roll(stage[t * per + j, :size, :], j * w, 1)
                     )
-                ref[t, TOP : TOP + deep, :] = v
+                ref[t, to : to + size, :] = v
     part = slide_low.shape[0]
     lane_p = lane_of((part, LANES))
     for p in range(LANES // EDGE):
@@ -345,32 +406,32 @@
         stage[0, p * part : (p + 1) * part, :] = jnp.where(
             lane_p < EDGE, up, jnp.where(lane_p >= LANES - EDGE, down, 0.0)
         )
-    for a, ref in enumerate(slides):
-        ref[tiles, TOP : TOP + deep, :] = stage[0, a * deep : (a + 1) * deep, :]
+    for ref, to, at, size in slides:
+        ref[tiles, to : to + size, :] = stage[0, at : at + size, :]
 
     lane = lane_of((8, LANES))
     row = row_of((8, LANES))
 
-    def y_of(t):
+    def y_of(t, lane):
         local = lane + t * LANES
         if t == tiles:
             local = jnp.where(lane < EDGE, local, lane - LANES)
         return local + b * tile_y
 
-    def y_in(t):
-        y = y_of(t)
+    def y_in(t, lane):
+        y = y_of(t, lane)
         return (y >= 0) & (y < cells_y) & ((lane < EDGE) | (lane >= LANES - EDGE))
 
-    def x_in(c):
-        x = row + (c * 8 - RIM) + g * tile_x
-        return (x >= 0) & (x < cells_x)
+    def x_masked(c, value):
+        if c[0] * 8 >= RIM and c[0] * 8 + c[1] <= RIM + tile_x:
+            return value
+        x = row_of((c[1], LANES)) + (c[0] * 8 - RIM) + g * tile_x
+        return jnp.where((x >= 0) & (x < cells_x), value, 0.0)
 
     def masked(c, t, value):
-        mine = c * 8 >= RIM and c * 8 + 8 <= RIM + tile_x
-        if not mine:
-            value = jnp.where(x_in(c), value, 0.0)
+        value = x_masked(c, value)
         if t == tiles:
-            value = jnp.where(y_in(t), value, 0.0)
+            value = jnp.where(y_in(t, lane_of((c[1], LANES))), value, 0.0)
         return value
 
     def coefficients(c, carry):
@@ -379,8 +440,8 @@
         x_ok = (x >= 0) & (x < cells_x)
         x_ends = 4.0 - (x == 0).astype(F32) - (x == cells_x - 1).astype(F32)
         for t in every:
-            y = y_of(t)
-            inside = x_ok & y_in(t) if t == tiles else x_ok
+            y = y_of(t, lane)
+            inside = x_ok & y_in(t, lane) if t == tiles else x_ok
             depth = jnp.where(inside, corner[t, at, :], 1.0)
             k = 9.0 / (depth * depth)
             p1 = 1.0 / (1.0 + 3.0 * k)
@@ -400,23 +461,40 @@
 
     def chunks(width):
         width = min(width, RIM)
-        return range((RIM - width) // 8, -(-(RIM + tile_x + width) // 8))
+        first, stop = (RIM - width) // 8, -(-(RIM + tile_x + width) // 8)
+        return [(c, min(GROUP, stop - c) * 8) for c in range(first, stop, GROUP)]
 
     def rows(ref, t, c, by=0):
-        return ref[t, TOP + c * 8 + by : TOP + c * 8 + by + 8, :]
+        at = TOP + c[0] * 8 + by
+        return ref[t, at : at + c[1], :]
 
     def put(ref, t, c, value):
-        ref[t, TOP + c * 8 : TOP + c * 8 + 8, :] = value
+        at = TOP + c[0] * 8
+        ref[t, at : at + c[1], :] = value
 
     def around(ref, c, reach):
-        mid = [rows(ref, t, c) for t in every]
-        fore = [pltpu.roll(v, reach, 1) for v in mid]
-        back = [pltpu.roll(v, LANES - reach, 1) for v in mid]
-        ring = []
-        for t in every:
-            west = jnp.where(lane < reach, fore[t - 1], fore[t])
-            east = jnp.where(lane >= LANES - reach, back[(t + 1) % (tiles + 1)], back[t])
-            ring.append((west + east) + (rows(ref, t, c, -reach) + rows(ref, t, c, reach)))
+        lane_c = lane_of((c[1], LANES))
+        mids, fores, backs = {}, {}, {}
+
+        def mid(t):
+            t = t % (tiles + 1)
+            if t not in mids:
+                mids[t] = rows(ref, t, c)
+            return mids[t]
+
+        def rolled(cache, t, by):
+            t = t % (tiles + 1)
+            if t not in cache:
+                cache[t] = pltpu.roll(mid(t), by, 1)
+            return cache[t]
+
+        def ring(t):
+            fore = functools.partial(rolled, fores, by=reach)
+            back = functools.partial(rolled, backs, by=LANES - reach)
+            west = jnp.where(lane_c < reach, fore(t - 1), fore(t))
+            east = jnp.where(lane_c >= LANES - reach, back(t + 1), back(t))
+            return (west + east) + (rows(ref, t, c, -reach) + rows(ref, t, c, reach))
+
         return mid, ring
 
     def solve(t, c, g1, g2, g3, out):
@@ -449,21 +527,17 @@
                 m_lo, m_hi = rows(m_now, t, c, -1), rows(m_now, t, c, 1)
                 h_lo, h_hi = rows(h_now, t, c, -1), rows(h_now, t, c, 1)
                 fresh = 0.5 * (h_lo + h_hi) - 0.5 * COURANT * (m_hi - m_lo)
-                mine = c * 8 >= RIM and c * 8 + 8 <= RIM + tile_x
-                if not mine:
-                    fresh = jnp.where(x_in(c), fresh, 0.0)
+                fresh = x_masked(c, fresh)
                 put(rise, t, c, fresh - h)
                 if moving:
                     q_lo, q_hi = rows(qs, t, c, -1), rows(qs, t, c, 1)
                     moved = (0.5 * (m_lo + m_hi) - 0.5 * COURANT * (q_hi - q_lo)) + rows(m_new, t, c)
-                    if not mine:
-                        moved = jnp.where(x_in(c), moved, 0.0)
                     put(h_new, t, c, fresh)
-                    put(m_new, t, c, moved)
+                    put(m_new, t, c, x_masked(c, moved))
         for c in chunks(reach - 2):
             mid, ring = around(eta, c, 2)
             for t in every:
-                push = GRAVITY_PUSH * (ring[t] - rows(corner, t, c) * mid[t])
+                push = GRAVITY_PUSH * (ring(t) - rows(corner, t, c) * mid(t))
                 up = rows(rise, t, c)
                 vector = []
                 for k in range(LAYERS):
@@ -474,28 +548,36 @@
                     vector.append(s)
                 if level == 0:
                     solve(t, c, *vector, pb)
-        done = 1 if level == 0 else 0
-        for sweep in range(done, SWEEPS):
-            old, new = (pa, pb) if sweep % 2 == 0 else (pb, pa)
-            for c in chunks(reach - 2 - sweep):
+
+        def sweep(old, new, width):
+            for c in chunks(width):
                 rings = [around(old.at[k], c, 1)[1] for k in range(LAYERS)]
                 for t in every:
-                    solve(t, c, *(rings[k][t] + rows(src.at[k], t, c) for k in range(LAYERS)), new)
-        press = pa if SWEEPS % 2 == 0 else pb
+                    solve(t, c, *(rings[k](t) + rows(src.at[k], t, c) for k in range(LAYERS)), new)
+
+        pairs = SWEEPS // 2
+        if level == 0:
+            sweep(pb, pa, reach - 3)
+            pairs -= 1
+
+        def two(i, carry):
+            sweep(pa, pb, reach - 2)
+            sweep(pb, pa, reach - 3)
+            return carry
+
+        lax.fori_loop(0, pairs, two, 0)
+        press = pa
         for c in chunks(reach - STEP):
-            flow = None
-            for k in range(LAYERS):
-                mid, ring = around(press.at[k], c, 2)
-                ds = [
-                    rows(div.at[k], t, c) - SPREAD * (ring[t] - rows(corner, t, c) * mid[t])
-                    for t in every
-                ]
-                if moving:
-                    for t in every:
-                        put(div.at[k], t, c, ds[t])
-                flow = ds if flow is None else [f + d for f, d in zip(flow, ds)]
+            stencils = [around(press.at[k], c, 2) for k in range(LAYERS)]
             for t in every:
-                change = rows(rise, t, c) - (0.25 * SURFACE_STEP) * flow[t]
+                flow = None
+                for k in range(LAYERS):
+                    mid, ring = stencils[k]
+                    d = rows(div.at[k], t, c) - SPREAD * (ring(t) - rows(corner, t, c) * mid(t))
+                    if moving:
+                        put(div.at[k], t, c, d)
+                    flow = d if flow is None else flow + d
+                change = rows(rise, t, c) - (0.25 * SURFACE_STEP) * flow
                 put(eta, t, c, rows(eta, t, c) + masked(c, t, change))
         for c in chunks(0):
             for t in range(tiles):
@@ -504,18 +586,14 @@
                     bottom = rows(load, t, c) + bottom
                 put(load, t, c, bottom * (1.0 / LEVELS) if level == LEVELS - 1 else bottom)
     for q in range(n):
-        for shift in range(n):
-
-            @pl.when(lax.rem(g + shift, n) == q)
-            def _():
-                turned = load[q * w // LANES, own : own + tile_x, :].T
-                loads[shift][...] = turned[q * w % LANES : q * w % LANES + w, :]
-
-    press = pa if SWEEPS % 2 == 0 else pb
+        turned = load[q * w // LANES, own : own + tile_x, :].T
+        bottoms[q] = turned[q * w % LANES : q * w % LANES + w, :]
+    for shift in range(n):
+        loads[shift][...] = bottoms[receiver(g, shift, n)]
     for t in range(tiles):
         fields_out[0, t] = eta[t, own : own + tile_x, :]
         for k in range(LAYERS):
-            fields_out[1 + k, t] = press[k, t, own : own + tile_x, :]
+            fields_out[1 + k, t] = pa[k, t, own : own + tile_x, :]
 
 
 def turn_kernel(fields, eta_out, press_out):
@@ -526,12 +604,12 @@
             press_out[k, rows, :] = fields[1 + k, i].T
 
 
-def place_load_kernel(n, where_ref, *refs):
+def place_load_kernel(n, *refs):
     parts, out = refs[:n], refs[n]
-    g = where_ref[0]
+    g = strip_place()
     tile_x = parts[0].shape[1]
     for shift in range(n):
-        col = pl.multiple_of(lax.rem(g - shift + n, n) * tile_x, LANES)
+        col = pl.multiple_of(sender(g, shift, n) * tile_x, LANES)
         out[:, pl.ds(col, tile_x)] = parts[shift][...]
 
 
@@ -553,9 +631,6 @@
     secs, gys = lax.axis_size("sec"), lax.axis_size("gy")
     nb = secs * gys
     along = ("sec", "gy")
-    g = lax.axis_index("gx")
-    b = lax.axis_index(along)
-    where = jnp.stack([g, b, jnp.int32(n), jnp.int32(nb)]).astype(jnp.int32)
     deep = tile_x + 2 * RIM
     tiles = tile_y // LANES + 1
     total = TOP + deep + TOP
@@ -566,15 +641,22 @@
     def turn(v, axis, count, by):
         return lax.ppermute(v, axis, [(i, (i + by) % count) for i in range(count)])
 
+    def across(v, shift):
+        pairs = [(i, i ^ shift if n & (n - 1) == 0 else (i + shift) % n) for i in range(n)]
+        return lax.ppermute(v, "gx", pairs)
+
+    strips = [padded(v) for v in (th, fp, mo, fr)]
+    block_rows = 3 * deep - 2 * TRIM
     blocks = call(
         functools.partial(pack_slide_kernel, n, tile_x),
-        [where],
-        [padded(v) for v in (th, fp, mo, fr)],
-        [(3 * deep, LANES)] * n,
+        [],
+        strips,
+        [(block_rows, LANES)] * n,
         [pltpu.VMEM((3, cells_x + 2 * RIM, LANES), F32)],
-        name="pack_slide",
-    )
-    blocks = [blocks[0]] + [turn(blocks[s], "gx", n, s) for s in range(1, n)]
+        room=63,
+        fetch=True,
+    )
+    blocks = [blocks[0]] + [across(blocks[s], s) for s in range(1, n)]
 
     edge_rows = 6 * EDGE + 8
     low, high, wide, edge_u = call(
@@ -583,17 +665,17 @@
         [surface, flux_x, flux_y, bathy_class],
         [(edge_rows, tile_x)] * 2 + [(5, tile_x, tile_y), (8, tile_y)],
         [pltpu.VMEM((LAYERS, tile_y + 16, tile_x), F32)],
-        name="pack_wave",
+        room=63,
+        fetch=True,
     )
     from_low = turn(high, along, nb, 1)
     from_high = turn(low, along, nb, -1)
     halo = (tiles * (5 * RIM + 4), LANES)
     wide, edge_u, send_a, send_b = call(
-        widen_wave_kernel,
-        [where],
+        functools.partial(widen_wave_kernel, nb),
+        [],
         [wide, edge_u, low, high, from_low, from_high],
         [(5, tiles, tile_x, LANES), (tiles, 8, LANES)] + [halo] * 2,
-        name="widen_wave",
     )
 
     def swap(v, first):
@@ -603,39 +685,39 @@
     got_a = swap(send_a, 0)
     got_b = swap(send_b, 1)
 
-    part = -(-3 * deep // (8 * (LANES // EDGE))) * 8
+    part = -(-block_rows // (8 * (LANES // EDGE))) * 8
     rows = part * (LANES // EDGE)
     slide_low, slide_high = call(
         functools.partial(slide_edge_kernel, n, w),
-        [where],
+        [],
         blocks,
         [(part, LANES)] * 2,
         [pltpu.VMEM((rows, LANES), F32)] * 2,
-        name="slide_edge",
     )
     slide_from_low = turn(slide_high, along, nb, 1)
     slide_from_high = turn(slide_low, along, nb, -1)
 
-    last_h, last_m = call(
+    devices = secs * n * gys
+    own_rows = cells_x // devices
+    state = pltpu.VMEM((2, cells_x + 16, LANES), F32)
+    (both,) = call(
         slide_kernel,
         [],
-        [padded(v) for v in (th, fp, mo, fr)],
-        [(cells_x, LANES)] * 2,
-        [pltpu.VMEM((LANES, cells_x), F32)] * 2,
-        name="slide",
-    )
-    devices = secs * n * gys
-    own_rows = cells_x // devices
-    both = jnp.stack([v[:, :w].reshape(devices, own_rows, w) for v in (last_h, last_m)], axis=1)
-    both = lax.all_to_all(both, ("sec", "gx", "gy"), split_axis=0, concat_axis=0, tiled=True)
-    both = both.reshape(secs, n, gys, 2, own_rows, w)
-    both = jnp.transpose(both, (3, 4, 0, 2, 1, 5)).reshape(2, own_rows, -1)
+        strips,
+        [(devices, 2, own_rows, LANES)],
+        [state, state] + [pltpu.VMEM((cells_x + 16, LANES), F32)] * 2,
+        room=63,
+        fetch=True,
+    )
+    both = lax.all_to_all(
+        both[..., :w], ("sec", "gx", "gy"), split_axis=0, concat_axis=0, tiled=True
+    )
 
     one = (tiles, total, LANES)
     stage_count = 1 if w == LANES else n
     results = call(
         functools.partial(wave_kernel, n, w, cells_x, nb * tile_y),
-        [where],
+        [],
         [wide, edge_u, got_a, got_b, slide_from_low, slide_from_high, *blocks],
         [(w, tile_x)] * n + [(4, tiles - 1, tile_x, LANES)],
         [
@@ -654,6 +736,7 @@
                 one,
                 one,
                 (tiles - 1, total, LANES),
+                (n, w, tile_x),
                 (stage_count, rows, LANES),
                 halo,
                 halo,
@@ -661,17 +744,26 @@
         ],
         flops=10**9,
         moved=10**7,
-        name="wave",
+        room=30,
     )
     loads, fields = results[:n], results[n]
-    parts = [loads[0]] + [turn(loads[s], "gx", n, s) for s in range(1, n)]
+    parts = [loads[0]] + [across(loads[s], s) for s in range(1, n)]
     surface_out, pressure_out = call(
-        turn_kernel, [], [fields], [(tile_y, tile_x), (LAYERS, tile_y, tile_x)], name="turn"
-    )
-    (bottom,) = call(
-        functools.partial(place_load_kernel, n), [where], parts, [(w, cells_x)], name="place_load"
-    )
-    return (surface_out, pressure_out, bottom[None, None], both[0], both[1])
+        turn_kernel, [], [fields], [(tile_y, tile_x), (LAYERS, tile_y, tile_x)]
+    )
+    if w % LANES == 0:
+        last_h, last_m = call(
+            functools.partial(place_slide_kernel, secs, n, gys),
+            [],
+            [both],
+            [(own_rows, devices * w)] * 2,
+        )
+    else:
+        both = both.reshape(secs, n, gys, 2, own_rows, w)
+        last_h, last_m = jnp.transpose(both, (3, 4, 0, 2, 1, 5)).reshape(2, own_rows, -1)
+    parts, last_h, last_m, surface_out = lax.optimization_barrier((parts, last_h, last_m, surface_out))
+    (bottom,) = call(functools.partial(place_load_kernel, n), [], parts, [(w, cells_x)])
+    return (surface_out, pressure_out, bottom[None, None], last_h, last_m)
 
 
 def solution(mesh):

time: 116 us -> 106 us (0.914)
  Pallas kernels: 43.6 us -> 32.7 us
  local copies, waits for them, and re-layouts: 4.93 us -> 8.37 us
  other arithmetic: 2.45 us -> 0 us
    ppermute x0 -> x6, waiting for transfers between devices: none -> 24.1 us  [across(): return lax.ppermute(v, 'gx', pairs)]
    ppermute x10 -> x4, waiting for transfers between devices: 35.1 us -> 11.2 us  [turn(): return lax.ppermute(v, axis, [(i, (i + by) % count) for i in range(count)])]
    ppermute x10 -> x4, starting transfers between devices: 19.3 us -> 5.41 us  [turn(): return lax.ppermute(v, axis, [(i, (i + by) % count) for i in range(count)])]
    ppermute x0 -> x6, starting transfers between devices: none -> 12.8 us  [across(): return lax.ppermute(v, 'gx', pairs)]
    pallas_call x8 -> x9, Pallas kernels: 43.6 us -> 32.7 us  [call(): pl.pallas_call(kernel, out_shape=[jax.ShapeDtypeStruct(s, F32) for s in o...]
    unnamed x24 -> x16, local copies, waits for them, and re-layouts: 2.93 us -> 8.37 us
    another operation x2 -> x0, other arithmetic: 2.45 us -> none  [the longest x1 1.85 us: shards(): jnp.stack([v[:, :w].reshape(devices, own_rows, w) for v in (last_h, last_...]
    squeeze x2 -> x0, local copies, waits for them, and re-layouts: 1.62 us -> none  [shards(): return (surface_out, pressure_out, bottom[None, None], both[0], both[1])]
  transfers between devices with their start and end apart: 13 -> 13, of which waited for: 8 -> 8; matrix products, arithmetic and copies ran while one was open for 1% -> 0% of each run, Pallas kernels for 31% -> 27%
where the time goes in v1:
time: 106 us
  waiting for transfers between devices  35.3 us (33%)
  Pallas kernels  32.7 us (31%)
  starting transfers between devices  28.7 us (27%)
  local copies, waits for them, and re-layouts  8.37 us (8%)
    pallas_call x9, Pallas kernels, call(): pl.pallas_call(kernel, out_shape=[jax.ShapeDtypeStruct(s, F32) for s in o...  32.7 us
    ppermute x6, waiting for transfers between devices, across(): return lax.ppermute(v, 'gx', pairs)  24.1 us
    ppermute x6, starting transfers between devices, across(): return lax.ppermute(v, 'gx', pairs)  12.8 us
    ppermute x4, waiting for transfers between devices, turn(): return lax.ppermute(v, axis, [(i, (i + by) % count) for i in range(count)])  11.2 us
    unnamed x16, local copies, waits for them, and re-layouts  8.37 us
    all_to_all x1, starting transfers between devices, shards(): lax.all_to_all(both[..., :w], ('sec', 'gx', 'gy'), split_axis=0, concat_a...  7.33 us
    ppermute x4, starting transfers between devices, turn(): return lax.ppermute(v, axis, [(i, (i + by) % count) for i in range(count)])  5.41 us
    ppermute x2, starting transfers between devices, swap(): return lax.ppermute(v, 'gx', pairs + [(j, i) for i, j in pairs])  3.19 us
  transfers between devices with their start and end apart: 13, of which 8 were waited for; matrix products, arithmetic and copies ran while one was open for 0% of the time, Pallas kernels for 27%

profile of v1, /device:TPU:0, one launch (start us, length us, event | category | flops | bytes accessed | tf_op | source)
XLA Modules:
  0.0 105.8 jit_solution(4435827402453085446)
XLA Ops:
  0.6 3.4 %shard_map.133 = f32[32,2,16,128]{3,2,1,0:T(8,128)} custom-call(f32[128,512]{1,0:T(8,128)} %bitcast.5, s32[128,512]{1,0:T(8,128)} %bitcast.7, f32[128,512]{1,0:T(8,128)} %bitcast.9, f32[128,512]{1,0:T(8,128)} %bitcast.11), custom_call_target="tpu_custom_call" | custom-call | flops 1000000 | bytes 1000000 | tf_op jit(solution)/shard_map/pallas_call | solution.py:65
  4.0 7.3 %all-to-all-start = ((f32[32,2,16,128]{3,2,1,0:T(8,128)}), f32[32,2,16,128]{3,2,1,0:T(8,128)S(1)}, u32[]{:S(2)}, u32[]{:S(2)}) async-start(f32[32,2,16,128]{3,2,1,0:T(8,128)} %shard_map.133), calls=%async_computation | async-start | bytes 1048576 | tf_op jit(solution)/shard_map/all_to_all | solution.py:712
  11.3 4.5 %shard_map.128 = (f32[200,128]{1,0:T(8,128)}, f32[200,128]{1,0:T(8,128)}, f32[5,128,512]{2,1,0:T(8,128)}, f32[8,512]{1,0:T(8,128)}) custom-call(f32[8]{0:T(128)} %refs_0_.1, f32[512,128]{1,0:T(8,128)} %refs_1_.1, f32[3,512,128]{2,1,0:T(8,128)} %refs_2_.1, f32[3,512,128]{2,1,0:T(8,128)} %refs_3_.1, s32[512,128]{1,0:T(8,128)} %refs_4_.1), custom_call_target="tpu_custom_call" | custom-call | flops 1000000 | bytes 1000000 | tf_op jit(solution)/shard_map/pallas_call | solution.py:65
  15.8 1.8 %collective-permute-start = (f32[200,128]{1,0:T(8,128)}, f32[200,128]{1,0:T(8,128)S(1)}, u32[]{:S(2)}, u32[]{:S(2)}) collective-permute-start(f32[200,128]{1,0:T(8,128)} %get-tuple-element.38.high), channel_id=1, source_target_pairs={{0,1},{1,2},{2,3},{3,16},{16,17},{17,18},{18,19},{19,0},{4,5},{5,6... | collective-permute-start | bytes 307208 | tf_op jit(solution)/shard_map/ppermute | solution.py:642
  17.6 0.9 collective-permute-start.1
  18.5 4.2 %collective-permute-done.from_low = f32[200,128]{1,0:T(8,128)S(1)} collective-permute-done((f32[200,128]{1,0:T(8,128)}, f32[200,128]{1,0:T(8,128)S(1)}, u32[]{:S(2)}, u32[]{:S(2)}) %collective-permute-start) | collective-permute-done | bytes 102432 | tf_op jit(solution)/shard_map/ppermute | solution.py:642
  22.7 3.6 %collective-permute-done.1.from_high = f32[200,128]{1,0:T(8,128)S(1)} collective-permute-done((f32[200,128]{1,0:T(8,128)}, f32[200,128]{1,0:T(8,128)S(1)}, u32[]{:S(2)}, u32[]{:S(2)}) %collective-permute-start.1) | collective-permute-done | bytes 102432 | tf_op jit(solution)/shard_map/ppermute | solution.py:642
  26.3 0.0 copy-start
  26.3 1.3 %copy-done = f32[5,128,512]{2,1,0:T(8,128)S(1)} copy-done((f32[5,128,512]{2,1,0:T(8,128)S(1)}, f32[5,128,512]{2,1,0:T(8,128)}, u32[]{:S(2)}) %copy-start) | copy-done | bytes 1310744
  27.7 0.0 copy-start.3
  27.7 0.9 copy-done.3
  28.5 0.0 copy-start.4
  28.5 0.9 copy-done.4
  29.4 0.0 copy-start.5
  29.4 0.7 copy-done.5
  30.2 1.0 shard_map.129
  31.2 0.0 copy-start.6
  31.2 1.2 %copy-done.6 = f32[5,5,128,128]{3,2,1,0:T(8,128)} copy-done((f32[5,5,128,128]{3,2,1,0:T(8,128)}, f32[5,5,128,128]{3,2,1,0:T(8,128)S(1)}, u32[]{:S(2)}) %copy-start.6) | copy-done | bytes 1638424
  32.4 1.8 %collective-permute-start.2 = (f32[720,128]{1,0:T(8,128)}, f32[720,128]{1,0:T(8,128)}, u32[]{:S(2)}, u32[]{:S(2)}) collective-permute-start(f32[720,128]{1,0:T(8,128)} %get-tuple-element.41), channel_id=1, source_target_pairs={{0,4},{8,12},{4,0},{12,8},{1,5},{9,13},{5,1},{13,9},{2,6},{10,14},... | collective-permute-start | bytes 1105928 | tf_op jit(solution)/shard_map/ppermute | solution.py:683
  34.2 1.4 %collective-permute-start.3 = (f32[720,128]{1,0:T(8,128)S(1)}, f32[720,128]{1,0:T(8,128)}, u32[]{:S(2)}, u32[]{:S(2)}) collective-permute-start(f32[720,128]{1,0:T(8,128)S(1)} %get-tuple-element.42), channel_id=1, source_target_pairs={{4,8},{8,4},{5,9},{9,5},{6,10},{10,6},{7,11},{11,7},{20,24},{24,20... | collective-permute-start | bytes 1105928 | tf_op jit(solution)/shard_map/ppermute | solution.py:683
  35.6 2.6 %shard_map.130 = (f32[536,128]{1,0:T(8,128)}, f32[536,128]{1,0:T(8,128)}, f32[536,128]{1,0:T(8,128)}, f32[536,128]{1,0:T(8,128)}) custom-call(f32[128,512]{1,0:T(8,128)} %bitcast.6, s32[128,512]{1,0:T(8,128)} %bitcast.8, f32[128,512]{1,0:T(8,128)} %bitcast.10, f32[128,512]{1,0:T(8,128)} %bitcast.12), custom_call_target="tpu_custom_call" | custom-call | flops 1000000 | bytes 1000000 | tf_op jit(solution)/shard_map/pallas_call | solution.py:65
  38.2 2.7 %collective-permute-start.4 = (f32[536,128]{1,0:T(8,128)}, f32[536,128]{1,0:T(8,128)S(1)}, u32[]{:S(2)}, u32[]{:S(2)}) collective-permute-start(f32[536,128]{1,0:T(8,128)} %get-tuple-element.44), channel_id=1, source_target_pairs={{0,4},{4,0},{8,12},{12,8},{1,5},{5,1},{9,13},{13,9},{2,6},{6,2},{1... | collective-permute-start | bytes 823304 | tf_op jit(solution)/shard_map/ppermute | solution.py:646
  40.9 0.0 collective-permute-start.5
  40.9 2.4 %collective-permute-start.6 = (f32[536,128]{1,0:T(8,128)}, f32[536,128]{1,0:T(8,128)S(1)}, u32[]{:S(2)}, u32[]{:S(2)}) collective-permute-start(f32[536,128]{1,0:T(8,128)} %get-tuple-element.46), channel_id=1, source_target_pairs={{0,12},{4,8},{8,4},{12,0},{1,13},{5,9},{9,5},{13,1},{2,14},{6,10},... | collective-permute-start | bytes 823304 | tf_op jit(solution)/shard_map/ppermute | solution.py:646
  43.3 9.3 %collective-permute-done.4.refs_1_.refs_7_ = f32[536,128]{1,0:T(8,128)S(1)} collective-permute-done((f32[536,128]{1,0:T(8,128)}, f32[536,128]{1,0:T(8,128)S(1)}, u32[]{:S(2)}, u32[]{:S(2)}) %collective-permute-start.4) | collective-permute-done | bytes 274464 | tf_op jit(solution)/shard_map/ppermute | solution.py:646
  52.6 12.2 %collective-permute-done.5.refs_2_.refs_8_ = f32[536,128]{1,0:T(8,128)S(1)} collective-permute-done((f32[536,128]{1,0:T(8,128)}, f32[536,128]{1,0:T(8,128)S(1)}, u32[]{:S(2)}, u32[]{:S(2)}) %collective-permute-start.5) | collective-permute-done | bytes 274464 | tf_op jit(solution)/shard_map/ppermute | solution.py:646
  64.8 0.0 collective-permute-done.6.refs_3_.refs_9_
  64.9 1.0 copy-done.1
  65.8 0.2 shard_map.131
  66.1 1.8 %collective-permute-start.7 = (f32[136,128]{1,0:T(8,128)S(1)}, f32[136,128]{1,0:T(8,128)S(1)}, u32[]{:S(2)}, u32[]{:S(2)}) collective-permute-start(f32[136,128]{1,0:T(8,128)S(1)} %get-tuple-element.47), channel_id=1, source_target_pairs={{0,1},{1,2},{2,3},{3,16},{16,17},{17,18},{18,19},{19,0},{4,5},{5,6... | collective-permute-start | bytes 208904 | tf_op jit(solution)/shard_map/ppermute | solution.py:642
  67.8 0.9 collective-permute-start.8
  68.8 2.0 %collective-permute-done.7.refs_4_ = f32[136,128]{1,0:T(8,128)S(1)} collective-permute-done((f32[136,128]{1,0:T(8,128)S(1)}, f32[136,128]{1,0:T(8,128)S(1)}, u32[]{:S(2)}, u32[]{:S(2)}) %collective-permute-start.7) | collective-permute-done | bytes 69664 | tf_op jit(solution)/shard_map/ppermute | solution.py:642
  70.7 1.4 %collective-permute-done.8.refs_5_ = f32[136,128]{1,0:T(8,128)S(1)} collective-permute-done((f32[136,128]{1,0:T(8,128)S(1)}, f32[136,128]{1,0:T(8,128)S(1)}, u32[]{:S(2)}, u32[]{:S(2)}) %collective-permute-start.8) | collective-permute-done | bytes 69664 | tf_op jit(solution)/shard_map/ppermute | solution.py:642
  72.1 0.0 collective-permute-done.2.refs_2_
  72.1 0.0 collective-permute-done.3.refs_3_
  72.1 1.0 copy-done.2
  73.1 1.4 %copy-done.7 = f32[5,5,128,128]{3,2,1,0:T(8,128)S(1)} copy-done((f32[5,5,128,128]{3,2,1,0:T(8,128)S(1)}, f32[5,5,128,128]{3,2,1,0:T(8,128)}, u32[]{:S(2)}) %copy-start.7) | copy-done | bytes 1638424
  74.5 18.2 %shard_map.132 = (f32[128,128]{1,0:T(8,128)S(1)}, f32[128,128]{1,0:T(8,128)S(1)}, f32[128,128]{1,0:T(8,128)S(1)}, f32[128,128]{1,0:T(8,128)S(1)}, f32[4,4,128,128]{3,2,1,0:T(8,128)S(1)}) custom-call(f32[5,5,128,128]{3,2,1,0:T(8,128)S(1)} %copy-done.7, f32[5,8,128]{2,1,0:T(8,128)S(1)} %get-tuple-element.40.refs_1_, ...), custom_call_target="tpu_custom_call" | custom-call | flops 1000000000 | bytes 10000000 | tf_op jit(solution)/shard_map/pallas_call | solution.py:65
  92.7 5.0 %collective-permute-start.9 = (f32[128,128]{1,0:T(8,128)S(1)}, f32[128,128]{1,0:T(8,128)S(1)}, u32[]{:S(2)}, u32[]{:S(2)}) collective-permute-start(f32[128,128]{1,0:T(8,128)S(1)} %get-tuple-element.50), channel_id=1, source_target_pairs={{0,4},{4,0},{8,12},{12,8},{1,5},{5,1},{9,13},{13,9},{2,6},{6,2},{1... | collective-permute-start | bytes 196616 | tf_op jit(solution)/shard_map/ppermute | solution.py:646
  97.7 1.2 %collective-permute-start.10 = (f32[128,128]{1,0:T(8,128)S(1)}, f32[128,128]{1,0:T(8,128)S(1)}, u32[]{:S(2)}, u32[]{:S(2)}) collective-permute-start(f32[128,128]{1,0:T(8,128)S(1)} %get-tuple-element.51), channel_id=1, source_target_pairs={{0,8},{4,12},{8,0},{12,4},{1,9},{5,13},{9,1},{13,5},{2,10},{6,14},... | collective-permute-start | bytes 196616 | tf_op jit(solution)/shard_map/ppermute | solution.py:646
  99.0 1.4 %collective-permute-start.11 = (f32[128,128]{1,0:T(8,128)S(1)}, f32[128,128]{1,0:T(8,128)S(1)}, u32[]{:S(2)}, u32[]{:S(2)}) collective-permute-start(f32[128,128]{1,0:T(8,128)S(1)} %get-tuple-element.52), channel_id=1, source_target_pairs={{0,12},{4,8},{8,4},{12,0},{1,13},{5,9},{9,5},{13,1},{2,14},{6,10},... | collective-permute-start | bytes 196616 | tf_op jit(solution)/shard_map/ppermute | solution.py:646
  100.3 1.3 %shard_map.135 = (f32[512,128]{1,0:T(8,128)}, f32[3,512,128]{2,1,0:T(8,128)}) custom-call(f32[4,4,128,128]{3,2,1,0:T(8,128)S(1)} %get-tuple-element.55.fields), custom_call_target="tpu_custom_call" | custom-call | flops 1000000 | bytes 1000000 | tf_op jit(solution)/shard_map/pallas_call | solution.py:65
  101.6 0.0 all-to-all-done.both
  101.6 0.8 shard_map.134
  102.5 0.0 collective-permute-done.9.refs_1_
  102.5 1.7 %collective-permute-done.10.refs_2_ = f32[128,128]{1,0:T(8,128)S(1)} collective-permute-done((f32[128,128]{1,0:T(8,128)S(1)}, f32[128,128]{1,0:T(8,128)S(1)}, u32[]{:S(2)}, u32[]{:S(2)}) %collective-permute-start.10) | collective-permute-done | bytes 65568 | tf_op jit(solution)/shard_map/ppermute | solution.py:646
  104.2 0.8 collective-permute-done.11.refs_3_
  105.0 0.7 shard_map.136
  (3 shorter events, 0.0 us)
Async XLA Ops:
  4.0 97.6 %all-to-all-start = ((f32[32,2,16,128]{3,2,1,0:T(8,128)}), f32[32,2,16,128]{3,2,1,0:T(8,128)S(1)}, u32[]{:S(2)}, u32[]{:S(2)}) async-start(f32[32,2,16,128]{3,2,1,0:T(8,128)} %shard_map.133), calls=%async_computation | async-start | bytes 1048576 | tf_op jit(solution)/shard_map/all_to_all | solution.py:712
  15.8 6.9 %collective-permute-start = (f32[200,128]{1,0:T(8,128)}, f32[200,128]{1,0:T(8,128)S(1)}, u32[]{:S(2)}, u32[]{:S(2)}) collective-permute-start(f32[200,128]{1,0:T(8,128)} %get-tuple-element.38.high), channel_id=1, source_target_pairs={{0,1},{1,2},{2,3},{3,16},{16,17},{17,18},{18,19},{19,0},{4,5},{5,6... | collective-permute-start | bytes 307208 | tf_op jit(solution)/shard_map/ppermute | solution.py:642
  17.6 8.7 %collective-permute-start.1 = (f32[200,128]{1,0:T(8,128)}, f32[200,128]{1,0:T(8,128)S(1)}, u32[]{:S(2)}, u32[]{:S(2)}) collective-permute-start(f32[200,128]{1,0:T(8,128)} %get-tuple-element.37.low), channel_id=1, source_target_pairs={{0,19},{1,0},{2,1},{3,2},{16,3},{17,16},{18,17},{19,18},{4,23},{5,... | collective-permute-start | bytes 307208 | tf_op jit(solution)/shard_map/ppermute | solution.py:642
  26.3 1.3 %copy-start = (f32[5,128,512]{2,1,0:T(8,128)S(1)}, f32[5,128,512]{2,1,0:T(8,128)}, u32[]{:S(2)}) copy-start(f32[5,128,512]{2,1,0:T(8,128)} %get-tuple-element.35.wide) | copy-start | bytes 3932164
  27.7 0.9 copy-start.3
  28.5 0.9 copy-start.4
  29.4 0.7 copy-start.5
  31.2 1.2 %copy-start.6 = (f32[5,5,128,128]{3,2,1,0:T(8,128)}, f32[5,5,128,128]{3,2,1,0:T(8,128)S(1)}, u32[]{:S(2)}) copy-start(f32[5,5,128,128]{3,2,1,0:T(8,128)S(1)} %get-tuple-element.39.refs_0_) | copy-start | bytes 4915204
  32.4 39.7 %collective-permute-start.2 = (f32[720,128]{1,0:T(8,128)}, f32[720,128]{1,0:T(8,128)}, u32[]{:S(2)}, u32[]{:S(2)}) collective-permute-start(f32[720,128]{1,0:T(8,128)} %get-tuple-element.41), channel_id=1, source_target_pairs={{0,4},{8,12},{4,0},{12,8},{1,5},{9,13},{5,1},{13,9},{2,6},{10,14},... | collective-permute-start | bytes 1105928 | tf_op jit(solution)/shard_map/ppermute | solution.py:683
  34.2 38.0 %collective-permute-start.3 = (f32[720,128]{1,0:T(8,128)S(1)}, f32[720,128]{1,0:T(8,128)}, u32[]{:S(2)}, u32[]{:S(2)}) collective-permute-start(f32[720,128]{1,0:T(8,128)S(1)} %get-tuple-element.42), channel_id=1, source_target_pairs={{4,8},{8,4},{5,9},{9,5},{6,10},{10,6},{7,11},{11,7},{20,24},{24,20... | collective-permute-start | bytes 1105928 | tf_op jit(solution)/shard_map/ppermute | solution.py:683
  38.2 14.5 %collective-permute-start.4 = (f32[536,128]{1,0:T(8,128)}, f32[536,128]{1,0:T(8,128)S(1)}, u32[]{:S(2)}, u32[]{:S(2)}) collective-permute-start(f32[536,128]{1,0:T(8,128)} %get-tuple-element.44), channel_id=1, source_target_pairs={{0,4},{4,0},{8,12},{12,8},{1,5},{5,1},{9,13},{13,9},{2,6},{6,2},{1... | collective-permute-start | bytes 823304 | tf_op jit(solution)/shard_map/ppermute | solution.py:646
  40.9 24.0 %collective-permute-start.5 = (f32[536,128]{1,0:T(8,128)}, f32[536,128]{1,0:T(8,128)S(1)}, u32[]{:S(2)}, u32[]{:S(2)}) collective-permute-start(f32[536,128]{1,0:T(8,128)} %get-tuple-element.45), channel_id=1, source_target_pairs={{0,8},{4,12},{8,0},{12,4},{1,9},{5,13},{9,1},{13,5},{2,10},{6,14},... | collective-permute-start | bytes 823304 | tf_op jit(solution)/shard_map/ppermute | solution.py:646
  40.9 24.0 %collective-permute-start.6 = (f32[536,128]{1,0:T(8,128)}, f32[536,128]{1,0:T(8,128)S(1)}, u32[]{:S(2)}, u32[]{:S(2)}) collective-permute-start(f32[536,128]{1,0:T(8,128)} %get-tuple-element.46), channel_id=1, source_target_pairs={{0,12},{4,8},{8,4},{12,0},{1,13},{5,9},{9,5},{13,1},{2,14},{6,10},... | collective-permute-start | bytes 823304 | tf_op jit(solution)/shard_map/ppermute | solution.py:646
  64.9 1.0 copy-start.1
  66.1 4.7 %collective-permute-start.7 = (f32[136,128]{1,0:T(8,128)S(1)}, f32[136,128]{1,0:T(8,128)S(1)}, u32[]{:S(2)}, u32[]{:S(2)}) collective-permute-start(f32[136,128]{1,0:T(8,128)S(1)} %get-tuple-element.47), channel_id=1, source_target_pairs={{0,1},{1,2},{2,3},{3,16},{16,17},{17,18},{18,19},{19,0},{4,5},{5,6... | collective-permute-start | bytes 208904 | tf_op jit(solution)/shard_map/ppermute | solution.py:642
  67.8 4.3 %collective-permute-start.8 = (f32[136,128]{1,0:T(8,128)S(1)}, f32[136,128]{1,0:T(8,128)S(1)}, u32[]{:S(2)}, u32[]{:S(2)}) collective-permute-start(f32[136,128]{1,0:T(8,128)S(1)} %get-tuple-element.48), channel_id=1, source_target_pairs={{0,19},{1,0},{2,1},{3,2},{16,3},{17,16},{18,17},{19,18},{4,23},{5,... | collective-permute-start | bytes 208904 | tf_op jit(solution)/shard_map/ppermute | solution.py:642
  72.1 1.0 copy-start.2
  73.1 1.4 %copy-start.7 = (f32[5,5,128,128]{3,2,1,0:T(8,128)S(1)}, f32[5,5,128,128]{3,2,1,0:T(8,128)}, u32[]{:S(2)}) copy-start(f32[5,5,128,128]{3,2,1,0:T(8,128)} %copy-done.6) | copy-start | bytes 4915204
  92.7 9.7 %collective-permute-start.9 = (f32[128,128]{1,0:T(8,128)S(1)}, f32[128,128]{1,0:T(8,128)S(1)}, u32[]{:S(2)}, u32[]{:S(2)}) collective-permute-start(f32[128,128]{1,0:T(8,128)S(1)} %get-tuple-element.50), channel_id=1, source_target_pairs={{0,4},{4,0},{8,12},{12,8},{1,5},{5,1},{9,13},{13,9},{2,6},{6,2},{1... | collective-permute-start | bytes 196616 | tf_op jit(solution)/shard_map/ppermute | solution.py:646
  97.7 6.5 %collective-permute-start.10 = (f32[128,128]{1,0:T(8,128)S(1)}, f32[128,128]{1,0:T(8,128)S(1)}, u32[]{:S(2)}, u32[]{:S(2)}) collective-permute-start(f32[128,128]{1,0:T(8,128)S(1)} %get-tuple-element.51), channel_id=1, source_target_pairs={{0,8},{4,12},{8,0},{12,4},{1,9},{5,13},{9,1},{13,5},{2,10},{6,14},... | collective-permute-start | bytes 196616 | tf_op jit(solution)/shard_map/ppermute | solution.py:646
  99.0 6.1 %collective-permute-start.11 = (f32[128,128]{1,0:T(8,128)S(1)}, f32[128,128]{1,0:T(8,128)S(1)}, u32[]{:S(2)}, u32[]{:S(2)}) collective-permute-start(f32[128,128]{1,0:T(8,128)S(1)} %get-tuple-element.52), channel_id=1, source_target_pairs={{0,12},{4,8},{8,4},{12,0},{1,13},{5,9},{9,5},{13,1},{2,14},{6,10},... | collective-permute-start | bytes 196616 | tf_op jit(solution)/shard_map/ppermute | solution.py:646

commit v2 on v1

--- a/solution.py
+++ b/solution.py
@@ -95,6 +95,21 @@
 
 def row_of(shape):
     return lax.broadcasted_iota(jnp.int32, shape, len(shape) - 2)
+
+
+def halo_layout(tiles):
+    places, at = {}, 0
+    for t in range(tiles + 1):
+        for a in range(5):
+            size = RIM if a == 0 else RIM - 2
+            if t == tiles and a in (2, 4):
+                places[t, a] = places[t, a - 1]
+                continue
+            places[t, a] = (at, size)
+            at += size
+        places[t, "u"] = (at, 4)
+        at += 4
+    return places, -(-at // 8) * 8
 
 
 def pack_slide_kernel(n, tile_x, th, fp, mo, fr, *rest):
@@ -257,15 +272,24 @@
             out[a, tiles - 1] = out[a, tiles - 1] + jnp.where(lane == LANES - 1, fix, 0.0)
             out[a, 0] = out[a, 0] + jnp.where(lane == 0, fix, 0.0)
 
+    places, length = halo_layout(tiles)
+
     def fill(send, right):
+        send[length - 8 :, :] = jnp.zeros((8, LANES), F32)
         for t in range(tiles + 1):
             for a in range(5):
-                at = (t * 5 + a) * RIM
-                rows = slice(tile_x - RIM, tile_x) if right else slice(0, RIM)
-                send[at : at + RIM, :] = out[a, t, rows, :]
-            at = (tiles + 1) * 5 * RIM + t * 4
+                at, size = places[t, a]
+                rows = slice(tile_x - size, tile_x) if right else slice(0, size)
+                value = out[a, t, rows, :]
+                if t == tiles and a in (2, 4):
+                    middle = (lane_of(value.shape) >= EDGE) & (lane_of(value.shape) < LANES - EDGE)
+                    value = jnp.where(middle, pltpu.roll(value, LANES // 2, 1), out[a - 1, t, rows, :])
+                elif t == tiles and a in (1, 3):
+                    continue
+                send[at : at + size, :] = value
+            at, size = places[t, "u"]
             rows = slice(LAYERS, LAYERS + 4) if right else slice(0, 4)
-            send[at : at + 4, :] = out_u[t, rows, :]
+            send[at : at + size, :] = out_u[t, rows, :]
 
     even = lax.rem(g, 2) == 0
 
@@ -341,6 +365,7 @@
         left[...] = got_a[...]
         right[...] = got_b[...]
 
+    places, _ = halo_layout(tiles)
     blank = jnp.zeros((TOP, LANES), F32)
     for t in every:
         for ref in (eta, hs.at[0], hs.at[1], ms.at[0], ms.at[1], qs):
@@ -351,11 +376,18 @@
                 ref[t, :TOP, :] = blank
                 ref[t, total - TOP :, :] = blank
         for a, ref in enumerate((eta, div.at[0], div.at[1], div.at[2], corner)):
-            at = (t * 5 + a) * RIM
-            ref[t, own - RIM : own, :] = left[at : at + RIM, :]
+            at, size = places[t, a]
+            before, after = left[at : at + size, :], right[at : at + size, :]
+            if t == tiles and a in (2, 4):
+                before = pltpu.roll(before, LANES // 2, 1)
+                after = pltpu.roll(after, LANES // 2, 1)
+            if size < RIM:
+                ref[t, TOP : TOP + 8, :] = jnp.ones((8, LANES), F32)
+                ref[t, TOP + deep - 8 : TOP + deep, :] = jnp.ones((8, LANES), F32)
+            ref[t, own - size : own, :] = before
             ref[t, own : own + tile_x, :] = wide[a, t]
-            ref[t, own + tile_x : own + tile_x + RIM, :] = right[at : at + RIM, :]
-        base = (tiles + 1) * 5 * RIM + t * 4
+            ref[t, own + tile_x : own + tile_x + size, :] = after
+        base = places[t, "u"][0]
         end = own + tile_x
         for k in range(LAYERS):
             d = div.at[k]
@@ -665,12 +697,11 @@
         [surface, flux_x, flux_y, bathy_class],
         [(edge_rows, tile_x)] * 2 + [(5, tile_x, tile_y), (8, tile_y)],
         [pltpu.VMEM((LAYERS, tile_y + 16, tile_x), F32)],
-        room=63,
         fetch=True,
     )
     from_low = turn(high, along, nb, 1)
     from_high = turn(low, along, nb, -1)
-    halo = (tiles * (5 * RIM + 4), LANES)
+    halo = (halo_layout(tiles - 1)[1], LANES)
     wide, edge_u, send_a, send_b = call(
         functools.partial(widen_wave_kernel, nb),
         [],
@@ -706,7 +737,6 @@
         strips,
         [(devices, 2, own_rows, LANES)],
         [state, state] + [pltpu.VMEM((cells_x + 16, LANES), F32)] * 2,
-        room=63,
         fetch=True,
     )
     both = lax.all_to_all(

time: 106 us -> 85.8 us (0.81)
  waiting for transfers between devices: 35.3 us -> 21.7 us
  Pallas kernels: 32.7 us -> 27.2 us
  local copies, waits for them, and re-layouts: 8.37 us -> 6.21 us
    ppermute x4, waiting for transfers between devices: 11.2 us -> 3.33 us  [turn(): return lax.ppermute(v, axis, [(i, (i + by) % count) for i in range(count)])]
    ppermute x6, waiting for transfers between devices: 24.1 us -> 18.3 us  [across(): return lax.ppermute(v, 'gx', pairs)]
    pallas_call x9, Pallas kernels: 32.7 us -> 27.2 us  [call(): pl.pallas_call(kernel, out_shape=[jax.ShapeDtypeStruct(s, F32) for s in o...]
    unnamed x16 -> x24, local copies, waits for them, and re-layouts: 8.37 us -> 6.21 us
  transfers between devices with their start and end apart: 13 -> 13, of which waited for: 8 -> 5; matrix products, arithmetic and copies ran while one was open for 0% -> 0% of each run, Pallas kernels for 27% -> 28%
where the time goes in v2:
time: 85.8 us; the launch traced here: 85.5 us
  starting transfers between devices  29.6 us (34%)
  Pallas kernels  27.2 us (32%)
  waiting for transfers between devices  21.7 us (25%)
  local copies, waits for them, and re-layouts  6.21 us (7%)
    pallas_call x9, Pallas kernels, call(): pl.pallas_call(kernel, out_shape=[jax.ShapeDtypeStruct(s, F32) for s in o...  27.2 us
    ppermute x6, waiting for transfers between devices, across(): return lax.ppermute(v, 'gx', pairs)  18.3 us
    ppermute x6, starting transfers between devices, across(): return lax.ppermute(v, 'gx', pairs)  13.5 us
    all_to_all x1, starting transfers between devices, shards(): lax.all_to_all(both[..., :w], ('sec', 'gx', 'gy'), split_axis=0, concat_a...  7.33 us
    unnamed x24, local copies, waits for them, and re-layouts  6.21 us
    ppermute x4, starting transfers between devices, turn(): return lax.ppermute(v, axis, [(i, (i + by) % count) for i in range(count)])  5.35 us
    ppermute x2, starting transfers between devices, swap(): return lax.ppermute(v, 'gx', pairs + [(j, i) for i, j in pairs])  3.45 us
    ppermute x4, waiting for transfers between devices, turn(): return lax.ppermute(v, axis, [(i, (i + by) % count) for i in range(count)])  3.33 us
  transfers between devices with their start and end apart: 13, of which 5 were waited for; matrix products, arithmetic and copies ran while one was open for 0% of the time, Pallas kernels for 28%

profile of v2, /device:TPU:0, one launch (start us, length us, event | category | flops | bytes accessed | tf_op | source)
XLA Modules:
  0.0 85.5 jit_solution(11858786930711229635)
XLA Ops:
  0.6 0.0 copy-start.11
  0.6 0.0 copy-start.2
  0.7 0.9 %copy-done.2 = f32[1,1,128,512]{3,2,1,0:T(8,128)S(1)} copy-done((f32[1,1,128,512]{3,2,1,0:T(8,128)S(1)}, f32[1,1,128,512]{3,2,1,0:T(8,128)}, u32[]{:S(2)}) %copy-start.2) | copy-done | bytes 262168
  1.6 0.9 %copy-done.3 = s32[1,1,128,512]{3,2,1,0:T(8,128)S(1)} copy-done((s32[1,1,128,512]{3,2,1,0:T(8,128)S(1)}, s32[1,1,128,512]{3,2,1,0:T(8,128)}, u32[]{:S(2)}) %copy-start.3) | copy-done | bytes 262168
  2.6 0.9 %copy-done.4 = f32[1,1,128,512]{3,2,1,0:T(8,128)S(1)} copy-done((f32[1,1,128,512]{3,2,1,0:T(8,128)S(1)}, f32[1,1,128,512]{3,2,1,0:T(8,128)}, u32[]{:S(2)}) %copy-start.4) | copy-done | bytes 262168
  3.5 0.9 %copy-done.5 = f32[1,1,128,512]{3,2,1,0:T(8,128)S(1)} copy-done((f32[1,1,128,512]{3,2,1,0:T(8,128)S(1)}, f32[1,1,128,512]{3,2,1,0:T(8,128)}, u32[]{:S(2)}) %copy-start.5) | copy-done | bytes 262168
  4.5 2.3 %shard_map.133 = f32[32,2,16,128]{3,2,1,0:T(8,128)} custom-call(f32[128,512]{1,0:T(8,128)S(1)} %bitcast.6, s32[128,512]{1,0:T(8,128)S(1)} %bitcast.8, f32[128,512]{1,0:T(8,128)S(1)} %bitcast.10, f32[128,512]{1,0:T(8,128)S(1)} %bitcast.12), custom_call_target="tpu_custom_call" | custom-call | flops 1000000 | bytes 1000000 | tf_op jit(solution)/shard_map/pallas_call | solution.py:65
  6.7 7.3 %all-to-all-start = ((f32[32,2,16,128]{3,2,1,0:T(8,128)}), f32[32,2,16,128]{3,2,1,0:T(8,128)S(1)}, u32[]{:S(2)}, u32[]{:S(2)}) async-start(f32[32,2,16,128]{3,2,1,0:T(8,128)} %shard_map.133), calls=%async_computation | async-start | bytes 1048576 | tf_op jit(solution)/shard_map/all_to_all | solution.py:742
  14.1 0.0 copy-done.11
  14.1 0.0 copy-done.6
  14.1 0.0 copy-done.7
  14.1 0.0 copy-done.9
  14.1 0.0 copy-done.10
  14.1 1.9 %shard_map.128 = (f32[200,128]{1,0:T(8,128)S(1)}, f32[200,128]{1,0:T(8,128)S(1)}, f32[5,128,512]{2,1,0:T(8,128)S(1)}, f32[8,512]{1,0:T(8,128)S(1)}) custom-call(f32[8]{0:T(128)S(1)} %copy-done.11, f32[512,128]{1,0:T(8,128)S(1)} %copy-done.9, f32[3,512,128]{2,1,0:T(8,128)S(1)} %copy-done.6, f32[3,512,128]{2,1,0:T(8,128)S(1)} %copy-done.7, ...), custom_call_target="tpu_custom_call" | custom-call | flops 1000000 | bytes 1000000 | tf_op jit(solution)/shard_map/pallas_call | solution.py:65
  16.1 1.1 %copy-done = f32[5,128,512]{2,1,0:T(8,128)} copy-done((f32[5,128,512]{2,1,0:T(8,128)}, f32[5,128,512]{2,1,0:T(8,128)S(1)}, u32[]{:S(2)}) %copy-start) | copy-done | bytes 1310744
  17.1 1.8 %collective-permute-start = (f32[200,128]{1,0:T(8,128)S(1)}, f32[200,128]{1,0:T(8,128)S(1)}, u32[]{:S(2)}, u32[]{:S(2)}) collective-permute-start(f32[200,128]{1,0:T(8,128)S(1)} %get-tuple-element.38.high), channel_id=1, source_target_pairs={{0,1},{1,2},{2,3},{3,16},{16,17},{17,18},{18,19},{19,0},{4,5},{5,6... | collective-permute-start | bytes 307208 | tf_op jit(solution)/shard_map/ppermute | solution.py:674
  18.9 0.9 %collective-permute-start.1 = (f32[200,128]{1,0:T(8,128)S(1)}, f32[200,128]{1,0:T(8,128)S(1)}, u32[]{:S(2)}, u32[]{:S(2)}) collective-permute-start(f32[200,128]{1,0:T(8,128)S(1)} %get-tuple-element.37.low), channel_id=1, source_target_pairs={{0,19},{1,0},{2,1},{3,2},{16,3},{17,16},{18,17},{19,18},{4,23},{5,... | collective-permute-start | bytes 307208 | tf_op jit(solution)/shard_map/ppermute | solution.py:674
  19.8 2.6 %shard_map.130 = (f32[536,128]{1,0:T(8,128)}, f32[536,128]{1,0:T(8,128)}, f32[536,128]{1,0:T(8,128)}, f32[536,128]{1,0:T(8,128)}) custom-call(f32[128,512]{1,0:T(8,128)} %bitcast.5, s32[128,512]{1,0:T(8,128)} %bitcast.7, f32[128,512]{1,0:T(8,128)} %bitcast.9, f32[128,512]{1,0:T(8,128)} %bitcast.11), custom_call_target="tpu_custom_call" | custom-call | flops 1000000 | bytes 1000000 | tf_op jit(solution)/shard_map/pallas_call | solution.py:65
  22.3 1.8 %collective-permute-start.4 = (f32[536,128]{1,0:T(8,128)}, f32[536,128]{1,0:T(8,128)S(1)}, u32[]{:S(2)}, u32[]{:S(2)}) collective-permute-start(f32[536,128]{1,0:T(8,128)} %get-tuple-element.44), channel_id=1, source_target_pairs={{0,4},{4,0},{8,12},{12,8},{1,5},{5,1},{9,13},{13,9},{2,6},{6,2},{1... | collective-permute-start | bytes 823304 | tf_op jit(solution)/shard_map/ppermute | solution.py:678
  24.2 2.4 %collective-permute-start.5 = (f32[536,128]{1,0:T(8,128)}, f32[536,128]{1,0:T(8,128)S(1)}, u32[]{:S(2)}, u32[]{:S(2)}) collective-permute-start(f32[536,128]{1,0:T(8,128)} %get-tuple-element.45), channel_id=1, source_target_pairs={{0,8},{4,12},{8,0},{12,4},{1,9},{5,13},{9,1},{13,5},{2,10},{6,14},... | collective-permute-start | bytes 823304 | tf_op jit(solution)/shard_map/ppermute | solution.py:678
  26.6 0.2 collective-permute-start.6
  26.8 0.0 collective-permute-done.from_low
  26.8 0.0 collective-permute-done.1.from_high
  26.8 1.3 %copy-done.1 = f32[5,128,512]{2,1,0:T(8,128)S(1)} copy-done((f32[5,128,512]{2,1,0:T(8,128)S(1)}, f32[5,128,512]{2,1,0:T(8,128)}, u32[]{:S(2)}) %copy-start.1) | copy-done | bytes 1310744
  28.1 0.3 shard_map.129
  28.4 2.8 %collective-permute-start.2 = (f32[632,128]{1,0:T(8,128)S(1)}, f32[632,128]{1,0:T(8,128)S(1)}, u32[]{:S(2)}, u32[]{:S(2)}) collective-permute-start(f32[632,128]{1,0:T(8,128)S(1)} %get-tuple-element.41), channel_id=1, source_target_pairs={{0,4},{8,12},{4,0},{12,8},{1,5},{9,13},{5,1},{13,9},{2,6},{10,14},... | collective-permute-start | bytes 970760 | tf_op jit(solution)/shard_map/ppermute | solution.py:714
  31.2 0.7 collective-permute-start.3
  31.9 6.0 %collective-permute-done.4.refs_1_.refs_7_ = f32[536,128]{1,0:T(8,128)S(1)} collective-permute-done((f32[536,128]{1,0:T(8,128)}, f32[536,128]{1,0:T(8,128)S(1)}, u32[]{:S(2)}, u32[]{:S(2)}) %collective-permute-start.4) | collective-permute-done | bytes 274464 | tf_op jit(solution)/shard_map/ppermute | solution.py:678
  37.9 9.4 %collective-permute-done.5.refs_2_.refs_8_ = f32[536,128]{1,0:T(8,128)S(1)} collective-permute-done((f32[536,128]{1,0:T(8,128)}, f32[536,128]{1,0:T(8,128)S(1)}, u32[]{:S(2)}, u32[]{:S(2)}) %collective-permute-start.5) | collective-permute-done | bytes 274464 | tf_op jit(solution)/shard_map/ppermute | solution.py:678
  47.3 0.0 collective-permute-done.6.refs_3_.refs_9_
  47.3 0.2 shard_map.131
  47.6 1.5 %collective-permute-start.7 = (f32[136,128]{1,0:T(8,128)S(1)}, f32[136,128]{1,0:T(8,128)S(1)}, u32[]{:S(2)}, u32[]{:S(2)}) collective-permute-start(f32[136,128]{1,0:T(8,128)S(1)} %get-tuple-element.47), channel_id=1, source_target_pairs={{0,1},{1,2},{2,3},{3,16},{16,17},{17,18},{18,19},{19,0},{4,5},{5,6... | collective-permute-start | bytes 208904 | tf_op jit(solution)/shard_map/ppermute | solution.py:674
  49.1 1.2 %collective-permute-start.8 = (f32[136,128]{1,0:T(8,128)S(1)}, f32[136,128]{1,0:T(8,128)S(1)}, u32[]{:S(2)}, u32[]{:S(2)}) collective-permute-start(f32[136,128]{1,0:T(8,128)S(1)} %get-tuple-element.48), channel_id=1, source_target_pairs={{0,19},{1,0},{2,1},{3,2},{16,3},{17,16},{18,17},{19,18},{4,23},{5,... | collective-permute-start | bytes 208904 | tf_op jit(solution)/shard_map/ppermute | solution.py:674
  50.3 2.7 %collective-permute-done.7.refs_4_ = f32[136,128]{1,0:T(8,128)S(1)} collective-permute-done((f32[136,128]{1,0:T(8,128)S(1)}, f32[136,128]{1,0:T(8,128)S(1)}, u32[]{:S(2)}, u32[]{:S(2)}) %collective-permute-start.7) | collective-permute-done | bytes 69664 | tf_op jit(solution)/shard_map/ppermute | solution.py:674
  52.9 0.6 collective-permute-done.8.refs_5_
  53.6 0.0 collective-permute-done.2.refs_2_
  53.6 0.0 collective-permute-done.3.refs_3_
  53.6 17.1 %shard_map.132 = (f32[128,128]{1,0:T(8,128)S(1)}, f32[128,128]{1,0:T(8,128)S(1)}, f32[128,128]{1,0:T(8,128)S(1)}, f32[128,128]{1,0:T(8,128)S(1)}, f32[4,4,128,128]{3,2,1,0:T(8,128)S(1)}) custom-call(f32[5,5,128,128]{3,2,1,0:T(8,128)S(1)} %get-tuple-element.39.refs_0_, f32[5,8,128]{2,1,0:T(8,128)S(1)} %get-tuple-element.40.refs_1_, ...), custom_call_target="tpu_custom_call" | custom-call | flops 1000000000 | bytes 10000000 | tf_op jit(solution)/shard_map/pallas_call | solution.py:65
  70.7 6.6 %collective-permute-start.9 = (f32[128,128]{1,0:T(8,128)S(1)}, f32[128,128]{1,0:T(8,128)S(1)}, u32[]{:S(2)}, u32[]{:S(2)}) collective-permute-start(f32[128,128]{1,0:T(8,128)S(1)} %get-tuple-element.50), channel_id=1, source_target_pairs={{0,4},{4,0},{8,12},{12,8},{1,5},{5,1},{9,13},{13,9},{2,6},{6,2},{1... | collective-permute-start | bytes 196616 | tf_op jit(solution)/shard_map/ppermute | solution.py:678
  77.3 0.5 collective-permute-start.10
  77.7 2.0 %collective-permute-start.11 = (f32[128,128]{1,0:T(8,128)S(1)}, f32[128,128]{1,0:T(8,128)S(1)}, u32[]{:S(2)}, u32[]{:S(2)}) collective-permute-start(f32[128,128]{1,0:T(8,128)S(1)} %get-tuple-element.52), channel_id=1, source_target_pairs={{0,12},{4,8},{8,4},{12,0},{1,13},{5,9},{9,5},{13,1},{2,14},{6,10},... | collective-permute-start | bytes 196616 | tf_op jit(solution)/shard_map/ppermute | solution.py:678
  79.7 1.3 %shard_map.135 = (f32[512,128]{1,0:T(8,128)}, f32[3,512,128]{2,1,0:T(8,128)}) custom-call(f32[4,4,128,128]{3,2,1,0:T(8,128)S(1)} %get-tuple-element.55.fields), custom_call_target="tpu_custom_call" | custom-call | flops 1000000 | bytes 1000000 | tf_op jit(solution)/shard_map/pallas_call | solution.py:65
  81.0 0.0 all-to-all-done.both
  81.0 0.8 shard_map.134
  81.8 0.0 collective-permute-done.9.refs_1_
  81.8 2.9 %collective-permute-done.10.refs_2_ = f32[128,128]{1,0:T(8,128)S(1)} collective-permute-done((f32[128,128]{1,0:T(8,128)S(1)}, f32[128,128]{1,0:T(8,128)S(1)}, u32[]{:S(2)}, u32[]{:S(2)}) %collective-permute-start.10) | collective-permute-done | bytes 65568 | tf_op jit(solution)/shard_map/ppermute | solution.py:678
  84.7 0.0 collective-permute-done.11.refs_3_
  84.7 0.7 shard_map.136
  (11 shorter events, 0.0 us)
Async XLA Ops:
  0.6 13.5 %copy-start.11 = (f32[8]{0:T(128)S(1)}, f32[8]{0:T(128)}, u32[]{:S(2)}) copy-start(f32[8]{0:T(128)} %refs_0_.1) | copy-start | bytes 100
  0.6 1.0 %copy-start.2 = (f32[1,1,128,512]{3,2,1,0:T(8,128)S(1)}, f32[1,1,128,512]{3,2,1,0:T(8,128)}, u32[]{:S(2)}) copy-start(f32[1,1,128,512]{3,2,1,0:T(8,128)} %param.9) | copy-start | bytes 786436
  1.6 0.9 %copy-start.3 = (s32[1,1,128,512]{3,2,1,0:T(8,128)S(1)}, s32[1,1,128,512]{3,2,1,0:T(8,128)}, u32[]{:S(2)}) copy-start(s32[1,1,128,512]{3,2,1,0:T(8,128)} %param.10) | copy-start | bytes 786436
  2.6 0.9 %copy-start.4 = (f32[1,1,128,512]{3,2,1,0:T(8,128)S(1)}, f32[1,1,128,512]{3,2,1,0:T(8,128)}, u32[]{:S(2)}) copy-start(f32[1,1,128,512]{3,2,1,0:T(8,128)} %param.11) | copy-start | bytes 786436
  3.5 0.9 %copy-start.5 = (f32[1,1,128,512]{3,2,1,0:T(8,128)S(1)}, f32[1,1,128,512]{3,2,1,0:T(8,128)}, u32[]{:S(2)}) copy-start(f32[1,1,128,512]{3,2,1,0:T(8,128)} %param.12) | copy-start | bytes 786436
  4.5 9.6 %copy-start.6 = (f32[3,512,128]{2,1,0:T(8,128)S(1)}, f32[3,512,128]{2,1,0:T(8,128)}, u32[]{:S(2)}) copy-start(f32[3,512,128]{2,1,0:T(8,128)} %refs_2_.1) | copy-start | bytes 2359300
  4.5 9.7 %copy-start.7 = (f32[3,512,128]{2,1,0:T(8,128)S(1)}, f32[3,512,128]{2,1,0:T(8,128)}, u32[]{:S(2)}) copy-start(f32[3,512,128]{2,1,0:T(8,128)} %refs_3_.1) | copy-start | bytes 2359300
  4.5 9.7 %copy-start.9 = (f32[512,128]{1,0:T(8,128)S(1)}, f32[512,128]{1,0:T(8,128)}, u32[]{:S(2)}) copy-start(f32[512,128]{1,0:T(8,128)} %refs_1_.1) | copy-start | bytes 786436
  4.5 9.7 %copy-start.10 = (s32[512,128]{1,0:T(8,128)S(1)}, s32[512,128]{1,0:T(8,128)}, u32[]{:S(2)}) copy-start(s32[512,128]{1,0:T(8,128)} %refs_4_.1) | copy-start | bytes 786436
  6.7 74.2 %all-to-all-start = ((f32[32,2,16,128]{3,2,1,0:T(8,128)}), f32[32,2,16,128]{3,2,1,0:T(8,128)S(1)}, u32[]{:S(2)}, u32[]{:S(2)}) async-start(f32[32,2,16,128]{3,2,1,0:T(8,128)} %shard_map.133), calls=%async_computation | async-start | bytes 1048576 | tf_op jit(solution)/shard_map/all_to_all | solution.py:742
  16.1 1.1 %copy-start = (f32[5,128,512]{2,1,0:T(8,128)}, f32[5,128,512]{2,1,0:T(8,128)S(1)}, u32[]{:S(2)}) copy-start(f32[5,128,512]{2,1,0:T(8,128)S(1)} %get-tuple-element.35.wide) | copy-start | bytes 3932164
  17.1 9.7 %collective-permute-start = (f32[200,128]{1,0:T(8,128)S(1)}, f32[200,128]{1,0:T(8,128)S(1)}, u32[]{:S(2)}, u32[]{:S(2)}) collective-permute-start(f32[200,128]{1,0:T(8,128)S(1)} %get-tuple-element.38.high), channel_id=1, source_target_pairs={{0,1},{1,2},{2,3},{3,16},{16,17},{17,18},{18,19},{19,0},{4,5},{5,6... | collective-permute-start | bytes 307208 | tf_op jit(solution)/shard_map/ppermute | solution.py:674
  18.9 7.9 %collective-permute-start.1 = (f32[200,128]{1,0:T(8,128)S(1)}, f32[200,128]{1,0:T(8,128)S(1)}, u32[]{:S(2)}, u32[]{:S(2)}) collective-permute-start(f32[200,128]{1,0:T(8,128)S(1)} %get-tuple-element.37.low), channel_id=1, source_target_pairs={{0,19},{1,0},{2,1},{3,2},{16,3},{17,16},{18,17},{19,18},{4,23},{5,... | collective-permute-start | bytes 307208 | tf_op jit(solution)/shard_map/ppermute | solution.py:674
  22.3 15.5 %collective-permute-start.4 = (f32[536,128]{1,0:T(8,128)}, f32[536,128]{1,0:T(8,128)S(1)}, u32[]{:S(2)}, u32[]{:S(2)}) collective-permute-start(f32[536,128]{1,0:T(8,128)} %get-tuple-element.44), channel_id=1, source_target_pairs={{0,4},{4,0},{8,12},{12,8},{1,5},{5,1},{9,13},{13,9},{2,6},{6,2},{1... | collective-permute-start | bytes 823304 | tf_op jit(solution)/shard_map/ppermute | solution.py:678
  24.2 23.1 %collective-permute-start.5 = (f32[536,128]{1,0:T(8,128)}, f32[536,128]{1,0:T(8,128)S(1)}, u32[]{:S(2)}, u32[]{:S(2)}) collective-permute-start(f32[536,128]{1,0:T(8,128)} %get-tuple-element.45), channel_id=1, source_target_pairs={{0,8},{4,12},{8,0},{12,4},{1,9},{5,13},{9,1},{13,5},{2,10},{6,14},... | collective-permute-start | bytes 823304 | tf_op jit(solution)/shard_map/ppermute | solution.py:678
  26.6 20.7 %collective-permute-start.6 = (f32[536,128]{1,0:T(8,128)}, f32[536,128]{1,0:T(8,128)S(1)}, u32[]{:S(2)}, u32[]{:S(2)}) collective-permute-start(f32[536,128]{1,0:T(8,128)} %get-tuple-element.46), channel_id=1, source_target_pairs={{0,12},{4,8},{8,4},{12,0},{1,13},{5,9},{9,5},{13,1},{2,14},{6,10},... | collective-permute-start | bytes 823304 | tf_op jit(solution)/shard_map/ppermute | solution.py:678
  26.8 1.3 %copy-start.1 = (f32[5,128,512]{2,1,0:T(8,128)S(1)}, f32[5,128,512]{2,1,0:T(8,128)}, u32[]{:S(2)}) copy-start(f32[5,128,512]{2,1,0:T(8,128)} %copy-done) | copy-start | bytes 3932164
  28.1 19.2 %copy-start.8 = (f32[536,128]{1,0:T(8,128)S(1)}, f32[536,128]{1,0:T(8,128)}, u32[]{:S(2)}) copy-start(f32[536,128]{1,0:T(8,128)} %get-tuple-element.43.refs_0_.refs_6_) | copy-start | bytes 823300
  28.4 25.1 %collective-permute-start.2 = (f32[632,128]{1,0:T(8,128)S(1)}, f32[632,128]{1,0:T(8,128)S(1)}, u32[]{:S(2)}, u32[]{:S(2)}) collective-permute-start(f32[632,128]{1,0:T(8,128)S(1)} %get-tuple-element.41), channel_id=1, source_target_pairs={{0,4},{8,12},{4,0},{12,8},{1,5},{9,13},{5,1},{13,9},{2,6},{10,14},... | collective-permute-start | bytes 970760 | tf_op jit(solution)/shard_map/ppermute | solution.py:714
  31.2 22.4 %collective-permute-start.3 = (f32[632,128]{1,0:T(8,128)S(1)}, f32[632,128]{1,0:T(8,128)S(1)}, u32[]{:S(2)}, u32[]{:S(2)}) collective-permute-start(f32[632,128]{1,0:T(8,128)S(1)} %get-tuple-element.42), channel_id=1, source_target_pairs={{4,8},{8,4},{5,9},{9,5},{6,10},{10,6},{7,11},{11,7},{20,24},{24,20... | collective-permute-start | bytes 970760 | tf_op jit(solution)/shard_map/ppermute | solution.py:714
  47.6 5.4 %collective-permute-start.7 = (f32[136,128]{1,0:T(8,128)S(1)}, f32[136,128]{1,0:T(8,128)S(1)}, u32[]{:S(2)}, u32[]{:S(2)}) collective-permute-start(f32[136,128]{1,0:T(8,128)S(1)} %get-tuple-element.47), channel_id=1, source_target_pairs={{0,1},{1,2},{2,3},{3,16},{16,17},{17,18},{18,19},{19,0},{4,5},{5,6... | collective-permute-start | bytes 208904 | tf_op jit(solution)/shard_map/ppermute | solution.py:674
  49.1 4.5 %collective-permute-start.8 = (f32[136,128]{1,0:T(8,128)S(1)}, f32[136,128]{1,0:T(8,128)S(1)}, u32[]{:S(2)}, u32[]{:S(2)}) collective-permute-start(f32[136,128]{1,0:T(8,128)S(1)} %get-tuple-element.48), channel_id=1, source_target_pairs={{0,19},{1,0},{2,1},{3,2},{16,3},{17,16},{18,17},{19,18},{4,23},{5,... | collective-permute-start | bytes 208904 | tf_op jit(solution)/shard_map/ppermute | solution.py:674
  70.7 11.1 %collective-permute-start.9 = (f32[128,128]{1,0:T(8,128)S(1)}, f32[128,128]{1,0:T(8,128)S(1)}, u32[]{:S(2)}, u32[]{:S(2)}) collective-permute-start(f32[128,128]{1,0:T(8,128)S(1)} %get-tuple-element.50), channel_id=1, source_target_pairs={{0,4},{4,0},{8,12},{12,8},{1,5},{5,1},{9,13},{13,9},{2,6},{6,2},{1... | collective-permute-start | bytes 196616 | tf_op jit(solution)/shard_map/ppermute | solution.py:678
  77.3 7.5 %collective-permute-start.10 = (f32[128,128]{1,0:T(8,128)S(1)}, f32[128,128]{1,0:T(8,128)S(1)}, u32[]{:S(2)}, u32[]{:S(2)}) collective-permute-start(f32[128,128]{1,0:T(8,128)S(1)} %get-tuple-element.51), channel_id=1, source_target_pairs={{0,8},{4,12},{8,0},{12,4},{1,9},{5,13},{9,1},{13,5},{2,10},{6,14},... | collective-permute-start | bytes 196616 | tf_op jit(solution)/shard_map/ppermute | solution.py:678
  77.7 7.0 %collective-permute-start.11 = (f32[128,128]{1,0:T(8,128)S(1)}, f32[128,128]{1,0:T(8,128)S(1)}, u32[]{:S(2)}, u32[]{:S(2)}) collective-permute-start(f32[128,128]{1,0:T(8,128)S(1)} %get-tuple-element.52), channel_id=1, source_target_pairs={{0,12},{4,8},{8,4},{12,0},{1,13},{5,9},{9,5},{13,1},{2,14},{6,10},... | collective-permute-start | bytes 196616 | tf_op jit(solution)/shard_map/ppermute | solution.py:678
